TPU v7x, 32 devices: a whole 2x2x4 slice. The times are simulated.
32 devices in a mesh: ep: 8 (over z, y), dp: 4 (over x, core).
Axes of the slice: x: 2, y: 2, z: 4, core: 2. Of those that a mesh axis runs over, the one named last changes fastest.
Arguments:
- tokens: bfloat16 [1024, 2048], P(('ep', 'dp')), may hold values from -6 to 6
- cotangent: bfloat16 [1024, 2048], P(('ep', 'dp')), may hold values from -6 to 6
- expert_ids: int32 [1024, 8], P(('ep', 'dp')), may hold values from 0 to 7, as said below
- route_weights: bfloat16 [1024, 8], P(('ep', 'dp')), may hold values from 0.049804688 to 0.5
- w_gate: bfloat16 [8, 2048, 768], P('ep'), may hold values from -0.125 to 0.125
- w_up: bfloat16 [8, 2048, 768], P('ep'), may hold values from -0.125 to 0.125
- w_down: bfloat16 [8, 768, 2048], P('ep'), may hold values from -0.21875 to 0.21875
Outputs:
- grad_tokens: bfloat16 [1024, 2048], P(('ep', 'dp'))
- grad_route: bfloat16 [1024, 8], P(('ep', 'dp'))
- grad_gate: bfloat16 [8, 2048, 768], P('ep', 'dp')
- grad_up: bfloat16 [8, 2048, 768], P('ep', 'dp')
- grad_down: bfloat16 [8, 768, 2048], P('ep', None, 'dp')
Inputs may be any that keep to these rules, and one draw needn't show every extreme that they name: `expert_ids`: each token names 8 different experts. The tokens of one device name no expert more than 32 times; 1 expert, drawn from the seed, are named exactly 32 times by every device's tokens.
All inputs are finite; a program needn't handle non-finite values.
Results may differ from a plain program's by a relative error of at most 0.0095.
Values may be sent and summed in bfloat16 or wider, within the bound.
A program may use at most 128 MiB of HBM per device.

v0:
```python
import jax
import jax.numpy as jnp
from jax import lax
from jax.sharding import PartitionSpec as P

block_rows = 128
contract_last = (((1,), (1,)), ((), ()))
contract_first = (((0,), (0,)), ((), ()))


def silu_parts(gate_pre):
    sig = jax.nn.sigmoid(gate_pre)
    return (gate_pre * sig, sig * (1.0 + gate_pre * (1.0 - sig)))


def expert_pass(rows_x, rows_cot, rows_w, live_count, w_gate_one, w_up_one, w_down_one):
    total, model = rows_x.shape
    width = w_gate_one.shape[1]

    def step(index, carry):
        acc_gate, acc_up, acc_down, slot_grad, route_grad = carry
        start = index * block_rows
        tok = lax.dynamic_slice_in_dim(rows_x, start, block_rows, 0)
        cot = lax.dynamic_slice_in_dim(rows_cot, start, block_rows, 0)
        weight = lax.dynamic_slice_in_dim(rows_w, start, block_rows, 0).astype(jnp.float32)[:, None]
        gate_pre = jnp.dot(tok, w_gate_one, preferred_element_type=jnp.float32)
        up_pre = jnp.dot(tok, w_up_one, preferred_element_type=jnp.float32)
        act, slope = silu_parts(gate_pre)
        hidden = lax.optimization_barrier((act * up_pre).astype(jnp.bfloat16))
        back = lax.dot_general(cot, w_down_one, contract_last, preferred_element_type=jnp.float32)
        route_part = jnp.sum(hidden.astype(jnp.float32) * back, axis=1)
        scaled = weight * back
        grad_gate_pre = (scaled * up_pre * slope).astype(jnp.bfloat16)
        grad_up_pre = (scaled * act).astype(jnp.bfloat16)
        scaled_cot = (weight * cot.astype(jnp.float32)).astype(jnp.bfloat16)
        part = lax.dot_general(
            grad_gate_pre, w_gate_one, contract_last, preferred_element_type=jnp.float32
        )
        part = part + lax.dot_general(
            grad_up_pre, w_up_one, contract_last, preferred_element_type=jnp.float32
        )
        acc_gate = acc_gate + lax.dot_general(
            tok, grad_gate_pre, contract_first, preferred_element_type=jnp.float32
        )
        acc_up = acc_up + lax.dot_general(
            tok, grad_up_pre, contract_first, preferred_element_type=jnp.float32
        )
        acc_down = acc_down + lax.dot_general(
            hidden, scaled_cot, contract_first, preferred_element_type=jnp.float32
        )
        slot_grad = lax.dynamic_update_slice_in_dim(slot_grad, part, start, 0)
        route_grad = lax.dynamic_update_slice_in_dim(route_grad, route_part, start, 0)
        return (acc_gate, acc_up, acc_down, slot_grad, route_grad)

    init = (
        jnp.zeros((model, width), jnp.float32),
        jnp.zeros((model, width), jnp.float32),
        jnp.zeros((width, model), jnp.float32),
        jnp.zeros((total, model), jnp.float32),
        jnp.zeros((total,), jnp.float32),
    )
    block_count = (live_count + block_rows - 1) // block_rows
    return lax.fori_loop(0, block_count, step, init)


def body(tokens, cotangent, expert_ids, route_weights, w_gate, w_up, w_down):
    tok_count, topk = expert_ids.shape
    model = tokens.shape[1]
    experts = lax.axis_size("ep")
    capacity = min(tok_count, 2 * tok_count * topk // experts)
    slots = tok_count * topk
    row_total = experts * capacity
    flat_ids = expert_ids.reshape(slots)
    onehot = (flat_ids[:, None] == jnp.arange(experts, dtype=jnp.int32)[None, :]).astype(jnp.int32)
    position = jnp.sum((jnp.cumsum(onehot, axis=0) - 1) * onehot, axis=1)
    slot_ids = jnp.arange(slots, dtype=jnp.int32)
    source = (
        jnp.full((row_total,), slots, jnp.int32).at[flat_ids * capacity + position].set(slot_ids)
    )
    filled = source < slots
    source_token = jnp.where(filled, source // topk, tok_count)
    joined = jnp.concatenate([tokens, cotangent], axis=1)
    picked = jnp.take(joined, source_token, axis=0, mode="fill", fill_value=0)
    send_x = picked[:, :model].reshape(experts, capacity, model)
    send_cot = picked[:, model:].reshape(experts, capacity, model)
    send_w = jnp.take(
        route_weights.reshape(slots), jnp.where(filled, source, slots), mode="fill", fill_value=0
    ).reshape(experts, capacity)
    recv_x, recv_cot, recv_w = (
        lax.all_to_all(send_x, "ep", split_axis=0, concat_axis=0, tiled=True),
        lax.all_to_all(send_cot, "ep", split_axis=0, concat_axis=0, tiled=True),
        lax.all_to_all(send_w, "ep", split_axis=0, concat_axis=0, tiled=True),
    )
    flat_w = recv_w.reshape(row_total)
    live = (flat_w != 0).astype(jnp.int32)
    live_count = jnp.sum(live)
    place = jnp.where(live > 0, jnp.cumsum(live) - 1, row_total)
    anchor = (
        jnp.full((row_total,), row_total, jnp.int32)
        .at[place]
        .set(jnp.arange(row_total, dtype=jnp.int32), mode="drop")
    )
    recv_joined = jnp.concatenate(
        [recv_x.reshape(row_total, model), recv_cot.reshape(row_total, model)], axis=1
    )
    packed = jnp.take(recv_joined, anchor, axis=0, mode="fill", fill_value=0)
    pack_x = packed[:, :model]
    pack_cot = packed[:, model:]
    pack_w = jnp.take(flat_w, anchor, mode="fill", fill_value=0)
    w_gate_one = w_gate[0]
    w_up_one = w_up[0]
    w_down_one = w_down[0]
    acc_gate, acc_up, acc_down, slot_grad, route_grad = expert_pass(
        pack_x, pack_cot, pack_w, live_count, w_gate_one, w_up_one, w_down_one
    )
    slot_rows = jnp.take(slot_grad, place, axis=0, mode="fill", fill_value=0.0).astype(jnp.bfloat16)
    route_rows = jnp.take(route_grad, place, axis=0, mode="fill", fill_value=0.0).astype(
        jnp.bfloat16
    )
    back_x, back_route_rows = (
        lax.all_to_all(
            slot_rows.reshape(experts, capacity, model),
            "ep",
            split_axis=0,
            concat_axis=0,
            tiled=True,
        ),
        lax.all_to_all(
            route_rows.reshape(experts, capacity), "ep", split_axis=0, concat_axis=0, tiled=True
        ),
    )
    mine_rows = back_x[flat_ids, position].reshape(tok_count, topk, model)
    grad_tokens = jnp.sum(mine_rows.astype(jnp.float32), axis=1).astype(jnp.bfloat16)
    grad_route = back_route_rows[flat_ids, position].reshape(tok_count, topk)
    summed = (
        lax.psum_scatter(
            acc_gate[None].astype(jnp.bfloat16), "dp", scatter_dimension=1, tiled=True
        ).astype(jnp.float32),
        lax.psum_scatter(
            acc_up[None].astype(jnp.bfloat16), "dp", scatter_dimension=1, tiled=True
        ).astype(jnp.float32),
        lax.psum_scatter(
            acc_down[None].astype(jnp.bfloat16), "dp", scatter_dimension=2, tiled=True
        ).astype(jnp.float32),
    )
    return (
        grad_tokens,
        grad_route,
        summed[0].astype(jnp.bfloat16),
        summed[1].astype(jnp.bfloat16),
        summed[2].astype(jnp.bfloat16),
    )


def solution(mesh):
    return jax.shard_map(
        body,
        mesh=mesh,
        in_specs=(
            P(("ep", "dp"), None),
            P(("ep", "dp"), None),
            P(("ep", "dp"), None),
            P(("ep", "dp"), None),
            P("ep", None, None),
            P("ep", None, None),
            P("ep", None, None),
        ),
        out_specs=(
            P(("ep", "dp"), None),
            P(("ep", "dp"), None),
            P("ep", "dp", None),
            P("ep", "dp", None),
            P("ep", None, "dp"),
        ),
        check_vma=False,
    )
```

profile of v0, /device:TPU:0, one launch (start us, length us, event | category | flops | bytes accessed | tf_op | source)
XLA Modules:
  0.0 277.8 jit_solution(4663596518100540112)
XLA Ops:
  14.0 7.3 %all-to-all-start = ((bf16[8,1,32]{2,1,0:T(2,128)(2,1)}), bf16[8,1,32]{2,1,0:T(2,128)(2,1)S(1)}, u32[]{:S(2)}, u32[]{:S(2)}) async-start(bf16[8,1,32]{2,1,0:T(2,128)(2,1)} %all_to_all.28), calls=%async_computation | async-start | bytes 8192 | tf_op jit(solution)/shard_map/all_to_all | solution.py:92
  27.8 28.9 %all_to_all.34 = bf16[8,32,2048]{2,1,0:T(8,128)(2,1)S(1)} all-to-all(bf16[8,32,2048]{2,1,0:T(8,128)(2,1)S(1)} %bitcast.82), channel_id=1, replica_groups=mesh['ep'=8,'dp'=4] {'ep'}, dimensions={0} | all-to-all | bytes 2097152 | tf_op jit(solution)/shard_map/all_to_all | solution.py:91
  56.7 3.6 %all-to-all-start.1 = ((bf16[8,32,2048]{2,1,0:T(8,128)(2,1)}), bf16[8,32,2048]{2,1,0:T(8,128)(2,1)S(1)}, u32[]{:S(2)}, u32[]{:S(2)}) async-start(bf16[8,32,2048]{2,1,0:T(8,128)(2,1)} %bitcast.7), calls=%async_computation.1 | async-start | bytes 2097152 | tf_op jit(solution)/shard_map/all_to_all | solution.py:90
  66.1 19.6 %all-to-all-done.1 = bf16[8,32,2048]{2,1,0:T(8,128)(2,1)S(1)} async-done(((bf16[8,32,2048]{2,1,0:T(8,128)(2,1)}), bf16[8,32,2048]{2,1,0:T(8,128)(2,1)S(1)}, u32[]{:S(2)}, u32[]{:S(2)}) %all-to-all-start.1) | async-done | bytes 1048608 | tf_op jit(solution)/shard_map/all_to_all | solution.py:90
  88.1 3.2 %gather_fusion.1 = bf16[256,4096]{1,0:T(8,128)(2,1)} fusion(bf16[256,4096]{1,0:T(8,128)(2,1)S(1)} %pad_maximum_fusion, s32[1024]{0:T(1024)S(1)} %pad_clamp_fusion.1), kind=kCustom, calls=%fused_computation.3 | custom fusion | bytes 4195328 | tf_op jit(solution)/shard_map/jit(_take)/gather | solution.py:106
  94.5 3.1 %broadcast.272 = f32[2048,768]{1,0:T(8,128)} broadcast(f32[]{:T(128)} %constant.126.clone.1), dimensions={} | broadcast | bytes 6291460 | tf_op jit(solution)/shard_map/broadcast.8
  97.6 3.1 %broadcast.272.clone = f32[2048,768]{1,0:T(8,128)} broadcast(f32[]{:T(128)} %constant.126.clone.1), dimensions={} | broadcast | bytes 6291460 | tf_op jit(solution)/shard_map/broadcast.8
  100.7 3.4 %broadcast_in_dim.69 = f32[768,2048]{1,0:T(8,128)} broadcast(f32[]{:T(128)} %constant.126.clone.1), dimensions={} | broadcast | bytes 6291460 | tf_op jit(solution)/shard_map/broadcast_in_dim | solution.py:58
  105.2 42.5 %while.18 = (s32[]{:T(128)}, f32[2048,768]{1,0:T(8,128)}, f32[2048,768]{1,0:T(8,128)}, f32[768,2048]{1,0:T(8,128)}, bf16[256,2048]{1,0:T(8,128)(2,1)}, /*index=5...) while((s32[]{:T(128)}, f32[2048,768]{1,0:T(8,128)}, ...), condition=%wide.region_10.12_spmd, body=%wide.region_8.11_spmd.sunk | while | flops 3228860416 | bytes 225381488 | solution.py:63
  105.2 2.8 %fusion.75 = f32[128,768]{1,0:T(8,128)S(1)} fusion(bf16[2048,768]{1,0:T(8,128)(2,1)} %get-tuple-element.274, bf16[256,2048]{1,0:T(8,128)(2,1)} %get-tuple-element.269, s32[]{:T(128)S(6)} %select_n.216), kind=kOutput, calls=%fused_computation.28.clone.1 | convolution fusion | flops 402653184 | bytes 4063236 | tf_op jit(solution)/shard_map/while/body/dot_general | solution.py:26
  108.7 3.2 %multiply_convert_fusion.8 = (bf16[128,768]{1,0:T(8,128)(2,1)S(1)}, bf16[128,768]{1,0:T(8,128)(2,1)S(1)}, bf16[128,768]{1,0:T(8,128)(2,1)S(1)}, f32[128,768]{1,0:T(8,128)S(1)}) fusion(f32[128]{0:T(128)S(1)} %dynamic-slice_convert_fusion.2, f32[128,768]{1,0:T(8,128)S(1)} %fusion.75, f32[128,768]{1,0:T(8,128)S(1)} %fusion.76, ...), kind=kOutput, calls=%fused_computation.22.clone.1 | convolution fusion | flops 404226048 | bytes 5440004 | tf_op jit(solution)/shard_map/while/body/dot_general | solution.py:30
  113.1 2.8 %copy-done.4 = f32[768,2048]{1,0:T(8,128)} copy-done((f32[768,2048]{1,0:T(8,128)}, f32[768,2048]{1,0:T(8,128)S(1)}, u32[]{:S(2)}) %copy-start.4) | copy-done | bytes 6291480 | tf_op jit(solution)/shard_map/while
  129.9 3.2 %multiply_convert_fusion.8 = (bf16[128,768]{1,0:T(8,128)(2,1)S(1)}, bf16[128,768]{1,0:T(8,128)(2,1)S(1)}, bf16[128,768]{1,0:T(8,128)(2,1)S(1)}, f32[128,768]{1,0:T(8,128)S(1)}) fusion(f32[128]{0:T(128)S(1)} %dynamic-slice_convert_fusion.2, f32[128,768]{1,0:T(8,128)S(1)} %fusion.75, f32[128,768]{1,0:T(8,128)S(1)} %fusion.76, ...), kind=kOutput, calls=%fused_computation.22.clone.1 | convolution fusion | flops 404226048 | bytes 5440004 | tf_op jit(solution)/shard_map/while/body/dot_general | solution.py:30
  134.4 2.8 %copy-done.4 = f32[768,2048]{1,0:T(8,128)} copy-done((f32[768,2048]{1,0:T(8,128)}, f32[768,2048]{1,0:T(8,128)S(1)}, u32[]{:S(2)}) %copy-start.4) | copy-done | bytes 6291480 | tf_op jit(solution)/shard_map/while
  147.7 4.8 %convert_bitcast_fusion.2 = bf16[1,2048,768]{2,1,0:T(8,128)(2,1)} fusion(f32[2048,768]{1,0:T(8,128)} %get-tuple-element.80), kind=kLoop, calls=%fused_computation.41 | loop fusion | flops 1572864 | bytes 9437184 | tf_op jit(solution)/shard_map/convert_element_type | solution.py:137
  152.5 4.7 %convert_bitcast_fusion.1 = bf16[1,2048,768]{2,1,0:T(8,128)(2,1)} fusion(f32[2048,768]{1,0:T(8,128)} %get-tuple-element.81), kind=kLoop, calls=%fused_computation.40 | loop fusion | flops 1572864 | bytes 9437184 | tf_op jit(solution)/shard_map/convert_element_type | solution.py:140
  157.3 5.7 %convert_bitcast_fusion = bf16[1,768,2048]{2,1,0:T(8,128)(2,1)} fusion(f32[768,2048]{1,0:T(8,128)} %get-tuple-element.82), kind=kLoop, calls=%fused_computation.39 | loop fusion | flops 1572864 | bytes 9437184 | tf_op jit(solution)/shard_map/convert_element_type | solution.py:143
  168.3 3.3 %all-to-all-start.4 = ((bf16[8,1,32]{2,1,0:T(2,128)(2,1)}), bf16[8,1,32]{2,1,0:T(2,128)(2,1)S(1)}, u32[]{:S(2)}, u32[]{:S(2)}) async-start(bf16[8,1,32]{2,1,0:T(2,128)(2,1)} %copy.29), calls=%async_computation.4 | async-start | bytes 8192 | tf_op jit(solution)/shard_map/all_to_all | solution.py:128
  172.9 5.1 %all-to-all-done.4 = bf16[8,1,32]{2,1,0:T(2,128)(2,1)S(1)} async-done(((bf16[8,1,32]{2,1,0:T(2,128)(2,1)}), bf16[8,1,32]{2,1,0:T(2,128)(2,1)S(1)}, u32[]{:S(2)}, u32[]{:S(2)}) %all-to-all-start.4) | async-done | bytes 544 | tf_op jit(solution)/shard_map/all_to_all | solution.py:128
  178.0 3.8 %all-to-all-start.3 = ((bf16[8,32,2048]{2,1,0:T(8,128)(2,1)}), bf16[8,32,2048]{2,1,0:T(8,128)(2,1)S(1)}, u32[]{:S(2)}, u32[]{:S(2)}) async-start(bf16[8,32,2048]{2,1,0:T(8,128)(2,1)} %select_convert_fusion), calls=%async_computation.3 | async-start | bytes 2097152 | tf_op jit(solution)/shard_map/all_to_all | solution.py:121
  184.9 21.3 %all-to-all-done.3 = bf16[8,32,2048]{2,1,0:T(8,128)(2,1)S(1)} async-done(((bf16[8,32,2048]{2,1,0:T(8,128)(2,1)}), bf16[8,32,2048]{2,1,0:T(8,128)(2,1)S(1)}, u32[]{:S(2)}, u32[]{:S(2)}) %all-to-all-start.3) | async-done | bytes 1048608 | tf_op jit(solution)/shard_map/all_to_all | solution.py:121
  206.2 4.3 %gather_fusion.3 = bf16[256,2048]{1,0:T(8,128)(2,1)S(1)} fusion(bf16[8,32,2048]{2,1,0:T(8,128)(2,1)S(1)} %all-to-all-done.3, s32[256]{0:T(256)S(1)} %bitcast.78), kind=kCustom, calls=%fused_computation.5 | custom fusion | bytes 2099200 | tf_op jit(solution)/shard_map/gather | solution.py:132
  211.9 18.5 %reduce-scatter.6.cloned.1.call-done = bf16[1,512,768]{2,1,0:T(8,128)(2,1)} async-done(((bf16[1,2048,768]{2,1,0:T(8,128)(2,1)}), bf16[1,512,768]{2,1,0:T(8,128)(2,1)}) %reduce-scatter.6.cloned.1.call-update) | async-done | bytes 786448 | tf_op jit(solution)/shard_map/reduce_scatter | solution.py:139
  230.4 40.9 %reduce-scatter.8.cloned.1.call-done = bf16[1,768,512]{2,1,0:T(8,128)(2,1)} async-done(((bf16[1,768,2048]{2,1,0:T(8,128)(2,1)}), bf16[1,768,512]{2,1,0:T(8,128)(2,1)}) %reduce-scatter.8.cloned.1.call-update) | async-done | bytes 786448 | tf_op jit(solution)/shard_map/reduce_scatter | solution.py:142
  (159 shorter events, 63.5 us)
Async XLA Ops:
  14.0 13.7 %all-to-all-start = ((bf16[8,1,32]{2,1,0:T(2,128)(2,1)}), bf16[8,1,32]{2,1,0:T(2,128)(2,1)S(1)}, u32[]{:S(2)}, u32[]{:S(2)}) async-start(bf16[8,1,32]{2,1,0:T(2,128)(2,1)} %all_to_all.28), calls=%async_computation | async-start | bytes 8192 | tf_op jit(solution)/shard_map/all_to_all | solution.py:92
  56.7 29.1 %all-to-all-start.1 = ((bf16[8,32,2048]{2,1,0:T(8,128)(2,1)}), bf16[8,32,2048]{2,1,0:T(8,128)(2,1)S(1)}, u32[]{:S(2)}, u32[]{:S(2)}) async-start(bf16[8,32,2048]{2,1,0:T(8,128)(2,1)} %bitcast.7), calls=%async_computation.1 | async-start | bytes 2097152 | tf_op jit(solution)/shard_map/all_to_all | solution.py:90
  60.2 151.7 %reduce-scatter.4.cloned.1.call-start = ((), (), s32[]{:S(2)}) async-start(), calls=%async_computation.8 | async-start | bytes 3932160 | tf_op jit(solution)/shard_map/reduce_scatter | solution.py:136
  100.7 4.5 %copy-start = (bf16[1,2048,768]{2,1,0:T(8,128)(2,1)S(1)}, bf16[1,2048,768]{2,1,0:T(8,128)(2,1)}, u32[]{:S(2)}) copy-start(bf16[1,2048,768]{2,1,0:T(8,128)(2,1)} %param.16) | copy-start | bytes 9437188
  105.2 3.5 %copy-start.9 = (bf16[256,2048]{1,0:T(8,128)(2,1)S(1)}, bf16[256,2048]{1,0:T(8,128)(2,1)}, u32[]{:S(2)}) copy-start(bf16[256,2048]{1,0:T(8,128)(2,1)} %get-tuple-element.271) | copy-start | bytes 3145732 | tf_op jit(solution)/shard_map/while
  105.2 6.7 %slice-start.4 = ((s8[6291456]{0:T(1024)(128)(4,1)}), s8[4194304]{0:T(1024)(128)(4,1)S(1)}, s32[]{:S(2)}) async-start(s8[6291456]{0:T(1024)(128)(4,1)} %bitcast.74), calls=%async_computation.15 | async-start | bytes 8388608 | tf_op jit(solution)/shard_map/while
  108.0 3.9 %slice-start.5 = ((s8[6291456]{0:T(1024)(128)(4,1)}), s8[2097152]{0:T(1024)(128)(4,1)S(1)}, s32[]{:S(2)}) async-start(s8[6291456]{0:T(1024)(128)(4,1)} %bitcast.74), calls=%async_computation.16 | async-start | bytes 4194304 | tf_op jit(solution)/shard_map/while
  111.9 4.1 %slice-start.2 = ((s8[6291456]{0:T(1024)(128)(4,1)}), s8[4194304]{0:T(1024)(128)(4,1)S(1)}, s32[]{:S(2)}) async-start(s8[6291456]{0:T(1024)(128)(4,1)} %bitcast.72), calls=%async_computation.13 | async-start | bytes 8388608 | tf_op jit(solution)/shard_map/while
  111.9 4.3 %slice-start.3 = ((s8[6291456]{0:T(1024)(128)(4,1)}), s8[2097152]{0:T(1024)(128)(4,1)S(1)}, s32[]{:S(2)}) async-start(s8[6291456]{0:T(1024)(128)(4,1)} %bitcast.72), calls=%async_computation.14 | async-start | bytes 4194304 | tf_op jit(solution)/shard_map/while
  116.0 4.2 %slice-start = ((s8[6291456]{0:T(1024)(128)(4,1)}), s8[4194304]{0:T(1024)(128)(4,1)S(1)}, s32[]{:S(2)}) async-start(s8[6291456]{0:T(1024)(128)(4,1)} %bitcast.70), calls=%async_computation.11 | async-start | bytes 8388608 | tf_op jit(solution)/shard_map/while
  116.2 4.0 %slice-start.1 = ((s8[6291456]{0:T(1024)(128)(4,1)}), s8[2097152]{0:T(1024)(128)(4,1)S(1)}, s32[]{:S(2)}) async-start(s8[6291456]{0:T(1024)(128)(4,1)} %bitcast.70), calls=%async_computation.12 | async-start | bytes 4194304 | tf_op jit(solution)/shard_map/while
  122.1 3.1 %copy-start.2 = (f32[2048,768]{1,0:T(8,128)}, f32[2048,768]{1,0:T(8,128)S(1)}, u32[]{:S(2)}) copy-start(f32[2048,768]{1,0:T(8,128)S(1)} %convolution_add_fusion.7) | copy-start | bytes 18874372 | tf_op jit(solution)/shard_map/while
  126.4 3.5 %copy-start.9 = (bf16[256,2048]{1,0:T(8,128)(2,1)S(1)}, bf16[256,2048]{1,0:T(8,128)(2,1)}, u32[]{:S(2)}) copy-start(bf16[256,2048]{1,0:T(8,128)(2,1)} %get-tuple-element.271) | copy-start | bytes 3145732 | tf_op jit(solution)/shard_map/while
  126.4 6.7 %slice-start.4 = ((s8[6291456]{0:T(1024)(128)(4,1)}), s8[4194304]{0:T(1024)(128)(4,1)S(1)}, s32[]{:S(2)}) async-start(s8[6291456]{0:T(1024)(128)(4,1)} %bitcast.74), calls=%async_computation.15 | async-start | bytes 8388608 | tf_op jit(solution)/shard_map/while
  129.2 3.9 %slice-start.5 = ((s8[6291456]{0:T(1024)(128)(4,1)}), s8[2097152]{0:T(1024)(128)(4,1)S(1)}, s32[]{:S(2)}) async-start(s8[6291456]{0:T(1024)(128)(4,1)} %bitcast.74), calls=%async_computation.16 | async-start | bytes 4194304 | tf_op jit(solution)/shard_map/while
  133.1 4.1 %slice-start.2 = ((s8[6291456]{0:T(1024)(128)(4,1)}), s8[4194304]{0:T(1024)(128)(4,1)S(1)}, s32[]{:S(2)}) async-start(s8[6291456]{0:T(1024)(128)(4,1)} %bitcast.72), calls=%async_computation.13 | async-start | bytes 8388608 | tf_op jit(solution)/shard_map/while
  133.2 4.3 %slice-start.3 = ((s8[6291456]{0:T(1024)(128)(4,1)}), s8[2097152]{0:T(1024)(128)(4,1)S(1)}, s32[]{:S(2)}) async-start(s8[6291456]{0:T(1024)(128)(4,1)} %bitcast.72), calls=%async_computation.14 | async-start | bytes 4194304 | tf_op jit(solution)/shard_map/while
  137.2 4.2 %slice-start = ((s8[6291456]{0:T(1024)(128)(4,1)}), s8[4194304]{0:T(1024)(128)(4,1)S(1)}, s32[]{:S(2)}) async-start(s8[6291456]{0:T(1024)(128)(4,1)} %bitcast.70), calls=%async_computation.11 | async-start | bytes 8388608 | tf_op jit(solution)/shard_map/while
  137.5 4.0 %slice-start.1 = ((s8[6291456]{0:T(1024)(128)(4,1)}), s8[2097152]{0:T(1024)(128)(4,1)S(1)}, s32[]{:S(2)}) async-start(s8[6291456]{0:T(1024)(128)(4,1)} %bitcast.70), calls=%async_computation.12 | async-start | bytes 4194304 | tf_op jit(solution)/shard_map/while
  143.3 3.1 %copy-start.2 = (f32[2048,768]{1,0:T(8,128)}, f32[2048,768]{1,0:T(8,128)S(1)}, u32[]{:S(2)}) copy-start(f32[2048,768]{1,0:T(8,128)S(1)} %convolution_add_fusion.7) | copy-start | bytes 18874372 | tf_op jit(solution)/shard_map/while
  152.5 77.9 %reduce-scatter.6.cloned.1.call-start = ((), (), s32[]{:S(2)}) async-start(), calls=%async_computation.9 | async-start | bytes 3932160 | tf_op jit(solution)/shard_map/reduce_scatter | solution.py:139
  157.3 114.0 %reduce-scatter.8.cloned.1.call-start = ((), (), s32[]{:S(2)}) async-start(), calls=%async_computation.10 | async-start | bytes 3932160 | tf_op jit(solution)/shard_map/reduce_scatter | solution.py:142
  168.3 9.7 %all-to-all-start.4 = ((bf16[8,1,32]{2,1,0:T(2,128)(2,1)}), bf16[8,1,32]{2,1,0:T(2,128)(2,1)S(1)}, u32[]{:S(2)}, u32[]{:S(2)}) async-start(bf16[8,1,32]{2,1,0:T(2,128)(2,1)} %copy.29), calls=%async_computation.4 | async-start | bytes 8192 | tf_op jit(solution)/shard_map/all_to_all | solution.py:128
  178.0 28.2 %all-to-all-start.3 = ((bf16[8,32,2048]{2,1,0:T(8,128)(2,1)}), bf16[8,32,2048]{2,1,0:T(8,128)(2,1)S(1)}, u32[]{:S(2)}, u32[]{:S(2)}) async-start(bf16[8,32,2048]{2,1,0:T(8,128)(2,1)} %select_convert_fusion), calls=%async_computation.3 | async-start | bytes 2097152 | tf_op jit(solution)/shard_map/all_to_all | solution.py:121
  (14 other events, 28.5 us)
Sparse Core Ops, SparseCore 0:
  152.6 36.7 reduce-scatter.3
  192.5 37.8 reduce-scatter.5
  233.5 37.7 reduce-scatter.7
where the time goes:
time: 279 us; the launch traced here: 278 us
  waiting for transfers between devices  108 us (39%)
  local copies, waits for them, and re-layouts  58.3 us (21%)
  blocking collectives  28.9 us (10%)
  matrix products  25.3 us (9%)
  other arithmetic  24.7 us (9%)
  starting transfers between devices  18.1 us (6%)
  between operations  14.7 us (5%)
    reduce_scatter x1, waiting for transfers between devices, body(): lax.psum_scatter(acc_down[None].astype(jnp.bfloat16), 'dp', scatter_dimen...  40.9 us
    all_to_all x1, blocking collectives, body(): lax.all_to_all(send_cot, 'ep', split_axis=0, concat_axis=0, tiled=True)  28.9 us
    all_to_all x1, waiting for transfers between devices, body(): lax.all_to_all(slot_rows.reshape(experts, capacity, model), 'ep', split_a...  21.3 us
    all_to_all x1, waiting for transfers between devices, body(): lax.all_to_all(send_x, 'ep', split_axis=0, concat_axis=0, tiled=True)  19.6 us
    reduce_scatter x1, waiting for transfers between devices, body(): lax.psum_scatter(acc_up[None].astype(jnp.bfloat16), 'dp', scatter_dimensi...  18.5 us
    while x56, local copies, waits for them, and re-layouts  16.1 us
    all_to_all x1, starting transfers between devices, body(): lax.all_to_all(send_w, 'ep', split_axis=0, concat_axis=0, tiled=True)  7.31 us
    another operation x9, local copies, waits for them, and re-layouts  6.62 us
  transfers between devices with their start and end apart: 7, of which 6 were waited for; matrix products, arithmetic and copies ran while one was open for 12% of the time, Pallas kernels for 0%

commit v1 on v0

--- a/solution.py
+++ b/solution.py
@@ -63,7 +63,7 @@
     return lax.fori_loop(0, block_count, step, init)
 
 
-def body(tokens, cotangent, expert_ids, route_weights, w_gate, w_up, w_down):
+def routed_body(tokens, cotangent, expert_ids, route_weights, w_gate, w_up, w_down):
     tok_count, topk = expert_ids.shape
     model = tokens.shape[1]
     experts = lax.axis_size("ep")
@@ -152,6 +152,88 @@
     )
 
 
+def dense_weights(expert_ids, route_weights, experts):
+    named = expert_ids[:, :, None] == jnp.arange(experts, dtype=jnp.int32)[None, None, :]
+    weights = route_weights.astype(jnp.float32)[:, :, None]
+    return jnp.sum(jnp.where(named, weights, 0.0), axis=1)
+
+
+def pick_route(table, expert_ids):
+    experts = table.shape[0]
+    named = expert_ids[:, :, None] == jnp.arange(experts, dtype=jnp.int32)[None, None, :]
+    spread = table.astype(jnp.float32).T[:, None, :]
+    return jnp.sum(jnp.where(named, spread, 0.0), axis=2).astype(jnp.bfloat16)
+
+
+def dense_body(tokens, cotangent, expert_ids, route_weights, w_gate, w_up, w_down):
+    tok_count, topk = expert_ids.shape
+    model = tokens.shape[1]
+    experts = lax.axis_size("ep")
+    groups = lax.axis_size("dp")
+    width = w_gate.shape[2]
+    rows = experts * tok_count
+    w_gate_one = w_gate[0]
+    w_up_one = w_up[0]
+    w_down_one = w_down[0]
+    weights = dense_weights(expert_ids, route_weights, experts).astype(jnp.bfloat16)
+    weight = lax.all_to_all(weights.T, "ep", split_axis=0, concat_axis=0, tiled=True)
+    weight = weight.reshape(rows, 1).astype(jnp.float32)
+    tok = lax.all_gather(tokens, "ep", axis=0, tiled=True)
+    cot = lax.all_gather(cotangent, "ep", axis=0, tiled=True)
+    gate_pre = jnp.dot(tok, w_gate_one, preferred_element_type=jnp.float32)
+    up_pre = jnp.dot(tok, w_up_one, preferred_element_type=jnp.float32)
+    act, slope = silu_parts(gate_pre)
+    hidden = (act * up_pre).astype(jnp.bfloat16)
+    back = lax.dot_general(cot, w_down_one, contract_last, preferred_element_type=jnp.float32)
+    route_part = jnp.sum(hidden.astype(jnp.float32) * back, axis=1)
+    scaled = weight * back
+    grad_gate_pre = (scaled * up_pre * slope).astype(jnp.bfloat16)
+    grad_up_pre = (scaled * act).astype(jnp.bfloat16)
+    scaled_cot = (weight * cot.astype(jnp.float32)).astype(jnp.bfloat16)
+    part = lax.dot_general(
+        grad_gate_pre, w_gate_one, contract_last, preferred_element_type=jnp.float32
+    )
+    part = part + lax.dot_general(
+        grad_up_pre, w_up_one, contract_last, preferred_element_type=jnp.float32
+    )
+    grad_tokens = lax.psum_scatter(
+        part.astype(jnp.bfloat16), "ep", scatter_dimension=0, tiled=True
+    )
+    route_table = lax.all_to_all(
+        route_part.astype(jnp.bfloat16).reshape(experts, tok_count),
+        "ep",
+        split_axis=0,
+        concat_axis=0,
+        tiled=True,
+    )
+    grad_route = pick_route(route_table, expert_ids)
+    tok_cols = lax.all_to_all(tok, "dp", split_axis=1, concat_axis=0, tiled=True)
+    cot_cols = lax.all_to_all(scaled_cot, "dp", split_axis=1, concat_axis=0, tiled=True)
+    hidden_all = lax.all_gather(hidden, "dp", axis=0, tiled=True)
+    gate_all = lax.all_gather(grad_gate_pre, "dp", axis=0, tiled=True)
+    up_all = lax.all_gather(grad_up_pre, "dp", axis=0, tiled=True)
+    grad_gate = lax.dot_general(tok_cols, gate_all, contract_first, preferred_element_type=jnp.float32)
+    grad_up = lax.dot_general(tok_cols, up_all, contract_first, preferred_element_type=jnp.float32)
+    grad_down = lax.dot_general(
+        hidden_all, cot_cols, contract_first, preferred_element_type=jnp.float32
+    )
+    return (
+        grad_tokens,
+        grad_route,
+        grad_gate[None].astype(jnp.bfloat16),
+        grad_up[None].astype(jnp.bfloat16),
+        grad_down[None].astype(jnp.bfloat16),
+    )
+
+
+def body(tokens, cotangent, expert_ids, route_weights, w_gate, w_up, w_down):
+    tok_count, topk = expert_ids.shape
+    experts = lax.axis_size("ep")
+    whole = 2 * tok_count * topk // experts >= tok_count
+    chosen = dense_body if whole else routed_body
+    return chosen(tokens, cotangent, expert_ids, route_weights, w_gate, w_up, w_down)
+
+
 def solution(mesh):
     return jax.shard_map(
         body,

time: 279 us -> 252 us (0.903)
  waiting for transfers between devices: 108 us -> 172 us
  local copies, waits for them, and re-layouts: 58.3 us -> 15.5 us
  blocking collectives: 28.9 us -> 8.85 us
  other arithmetic: 24.7 us -> 5.91 us
  starting transfers between devices: 18.1 us -> 12.2 us
    all_gather x0 -> x5, waiting for transfers between devices: none -> 80.5 us  [the longest x1 44.4 us: dense_body(): tok = lax.all_gather(tokens, 'ep', axis=0, tiled=True)]
    all_to_all x1, blocking collectives: 28.9 us -> 8.85 us  [dense_body(): lax.all_to_all(weights.T, 'ep', split_axis=0, concat_axis=0, tiled=True)]
    gather x9 -> x0, local copies, waits for them, and re-layouts: 18.8 us -> none  [the longest x1 4.32 us: body(): mine_rows = back_x[flat_ids, position].reshape(tok_count, topk, model)]
    while x56 -> x0, local copies, waits for them, and re-layouts: 16.1 us -> none
    convert_element_type x9 -> x4, other arithmetic: 16.7 us -> 5.3 us  [the longest x1 2.89 us: dense_body(): grad_up_pre = (scaled * act).astype(jnp.bfloat16)]
    all_to_all x4 -> x3, waiting for transfers between devices: 48.2 us -> 37.7 us  [the longest x1 20.6 us: dense_body(): lax.all_to_all(scaled_cot, 'dp', split_axis=1, concat_axis=0, tiled=True)]
    reduce_scatter x3 -> x1, waiting for transfers between devices: 59.4 us -> 51.4 us  [dense_body(): lax.psum_scatter(part.astype(jnp.bfloat16), 'ep', scatter_dimension=0, ti...]
    another operation x9 -> x0, local copies, waits for them, and re-layouts: 6.62 us -> none
  transfers between devices with their start and end apart: 7 -> 9, of which waited for: 6 -> 6; matrix products, arithmetic and copies ran while one was open for 12% -> 16% of each run, Pallas kernels for 0% -> 0%
where the time goes in v1:
time: 252 us
  waiting for transfers between devices  172 us (68%)
  matrix products  23.5 us (9%)
  local copies, waits for them, and re-layouts  15.5 us (6%)
  between operations  14.2 us (6%)
  starting transfers between devices  12.2 us (5%)
  blocking collectives  8.85 us (4%)
  other arithmetic  5.91 us (2%)
    reduce_scatter x1, waiting for transfers between devices, dense_body(): lax.psum_scatter(part.astype(jnp.bfloat16), 'ep', scatter_dimension=0, ti...  51.4 us
    all_gather x1, waiting for transfers between devices, dense_body(): tok = lax.all_gather(tokens, 'ep', axis=0, tiled=True)  44.4 us
    all_gather x1, waiting for transfers between devices, dense_body(): cot = lax.all_gather(cotangent, 'ep', axis=0, tiled=True)  36 us
    all_to_all x1, waiting for transfers between devices, dense_body(): lax.all_to_all(scaled_cot, 'dp', split_axis=1, concat_axis=0, tiled=True)  20.6 us
    all_to_all x1, waiting for transfers between devices, dense_body(): lax.all_to_all(tok, 'dp', split_axis=1, concat_axis=0, tiled=True)  10.7 us
    all_to_all x1, blocking collectives, dense_body(): lax.all_to_all(weights.T, 'ep', split_axis=0, concat_axis=0, tiled=True)  8.85 us
    all_to_all x1, waiting for transfers between devices, dense_body(): lax.all_to_all(route_part.astype(jnp.bfloat16).reshape(experts, tok_count...  6.35 us
    unnamed x18, local copies, waits for them, and re-layouts  5.62 us
  transfers between devices with their start and end apart: 9, of which 6 were waited for; matrix products, arithmetic and copies ran while one was open for 16% of the time, Pallas kernels for 0%

profile of v1, /device:TPU:0, one launch (start us, length us, event | category | flops | bytes accessed | tf_op | source)
XLA Modules:
  0.0 251.8 jit_solution(8826791404832517851)
XLA Ops:
  8.7 44.4 %all-gather.8.cloned.1.call-done = bf16[256,2048]{1,0:T(8,128)(2,1)} async-done(((bf16[32,2048]{1,0:T(8,128)(2,1)}), bf16[256,2048]{1,0:T(8,128)(2,1)}) %all-gather.8.cloned.1.call-update) | async-done | bytes 1048592 | tf_op jit(solution)/shard_map/all_gather | solution.py:181
  53.2 3.2 %fusion.2 = f32[256,768]{1,0:T(8,128)} fusion(bf16[256,2048]{1,0:T(8,128)(2,1)} %all-gather.8.cloned.1.call-done, bf16[1,2048,768]{2,1,0:T(8,128)(2,1)S(1)} %copy-done), kind=kOutput, calls=%fused_computation.2 | convolution fusion | flops 805306368 | bytes 4980736 | tf_op jit(solution)/shard_map/dot_general | solution.py:183
  58.3 36.0 %all-gather.6.cloned.1.call-done = bf16[256,2048]{1,0:T(8,128)(2,1)} async-done(((bf16[32,2048]{1,0:T(8,128)(2,1)}), bf16[256,2048]{1,0:T(8,128)(2,1)}) %all-gather.6.cloned.1.call-update) | async-done | bytes 1048592 | tf_op jit(solution)/shard_map/all_gather | solution.py:182
  94.3 4.7 %multiply_reduce_fusion = (bf16[256]{0:T(256)(128)(2,1)S(1)}, bf16[256,768]{1,0:T(8,128)(2,1)}, f32[256,768]{1,0:T(8,128)}) fusion(f32[256,768]{1,0:T(8,128)} %fusion.6, f32[256,768]{1,0:T(8,128)} %fusion.2, bf16[256,2048]{1,0:T(8,128)(2,1)} %all-gather.6.cloned.1.call-done, bf16[1,768,2048]{2,1,0:T(8,128)(2,1)} %param.13), kind=kOutput, calls=%fused_computation.19 | convolution fusion | flops 807075584 | bytes 6947328 | tf_op jit(solution)/shard_map/dot_general | solution.py:187
  99.7 3.3 %all-to-all-start.1 = ((bf16[8,1,32]{2,1,0:T(2,128)(2,1)}), bf16[8,1,32]{2,1,0:T(2,128)(2,1)S(1)}, u32[]{:S(2)}, u32[]{:S(2)}) async-start(bf16[8,1,32]{2,1,0:T(2,128)(2,1)} %convert_element_type.112), calls=%async_computation.2 | async-start | bytes 8192 | tf_op jit(solution)/shard_map/all_to_all | solution.py:202
  103.1 6.4 %all-to-all-done.1 = bf16[8,1,32]{2,1,0:T(2,128)(2,1)S(1)} async-done(((bf16[8,1,32]{2,1,0:T(2,128)(2,1)}), bf16[8,1,32]{2,1,0:T(2,128)(2,1)S(1)}, u32[]{:S(2)}, u32[]{:S(2)}) %all-to-all-start.1) | async-done | bytes 544 | tf_op jit(solution)/shard_map/all_to_all | solution.py:202
  110.0 8.8 %all_to_all.53 = bf16[8,1,32]{2,1,0:T(2,128)(2,1)S(1)} all-to-all(bf16[8,1,32]{2,1,0:T(2,128)(2,1)S(1)} %copy.51), channel_id=1, replica_groups=mesh['ep'=8,'dp'=4] {'ep'}, dimensions={0} | all-to-all | bytes 1024 | tf_op jit(solution)/shard_map/all_to_all | solution.py:179
  119.0 2.9 %multiply_convert_fusion.2 = (bf16[256,768]{1,0:T(8,128)(2,1)}, bf16[256,768]{1,0:T(8,128)(2,1)}) fusion(f32[256,768]{1,0:T(8,128)} %get-tuple-element.41, f32[256]{0:T(256)S(1)} %reshape.52, f32[256,768]{1,0:T(8,128)} %fusion.2, f32[256,768]{1,0:T(8,128)} %fusion.6), kind=kLoop, calls=%fused_computation.21 | loop fusion | flops 2752512 | bytes 3146752 | tf_op jit(solution)/shard_map/convert_element_type | solution.py:191
  122.5 2.3 copy.53
  124.8 4.4 %all-to-all-start.2 = ((bf16[256,4,512]{0,2,1:T(8,128)(2,1)}), bf16[256,4,512]{0,2,1:T(8,128)(2,1)}, u32[]{:S(2)}, u32[]{:S(2)}) async-start(bf16[256,4,512]{0,2,1:T(8,128)(2,1)} %bitcast.54), calls=%async_computation.3 | async-start | bytes 2097152 | tf_op jit(solution)/shard_map/all_to_all | solution.py:210
  129.3 2.3 copy.55
  133.6 2.0 fusion.13
  135.6 2.4 multiply_convert_fusion
  138.0 10.7 %all-to-all-done.2 = bf16[256,4,512]{0,2,1:T(8,128)(2,1)} async-done(((bf16[256,4,512]{0,2,1:T(8,128)(2,1)}), bf16[256,4,512]{0,2,1:T(8,128)(2,1)}, u32[]{:S(2)}, u32[]{:S(2)}) %all-to-all-start.2) | async-done | bytes 1048608 | tf_op jit(solution)/shard_map/all_to_all | solution.py:210
  148.8 4.3 %all-to-all-start.3 = ((bf16[256,4,512]{0,2,1:T(8,128)(2,1)}), bf16[256,4,512]{0,2,1:T(8,128)(2,1)}, u32[]{:S(2)}, u32[]{:S(2)}) async-start(bf16[256,4,512]{0,2,1:T(8,128)(2,1)} %bitcast.55), calls=%async_computation.4 | async-start | bytes 2097152 | tf_op jit(solution)/shard_map/all_to_all | solution.py:211
  153.0 2.3 copy.54
  155.3 20.6 %all-to-all-done.3 = bf16[256,4,512]{0,2,1:T(8,128)(2,1)} async-done(((bf16[256,4,512]{0,2,1:T(8,128)(2,1)}), bf16[256,4,512]{0,2,1:T(8,128)(2,1)}, u32[]{:S(2)}, u32[]{:S(2)}) %all-to-all-start.3) | async-done | bytes 1048608 | tf_op jit(solution)/shard_map/all_to_all | solution.py:211
  176.0 2.3 copy.56
  178.3 3.6 %fusion.18 = bf16[1,768,512]{2,1,0:T(8,128)(2,1)} fusion(bf16[1024,768]{1,0:T(8,128)(2,1)} %all-gather.14.cloned.1.call-done, bf16[1024,512]{1,0:T(8,128)(2,1)} %bitcast.58), kind=kOutput, calls=%fused_computation.18 | convolution fusion | flops 805699584 | bytes 3407872 | tf_op jit(solution)/shard_map/dot_general | solution.py:217
  181.8 3.6 %fusion.16 = bf16[1,512,768]{1,2,0:T(8,128)(2,1)} fusion(bf16[1024,768]{1,0:T(8,128)(2,1)} %all-gather.10.cloned.1.call-done, bf16[1024,512]{1,0:T(8,128)(2,1)} %bitcast.56), kind=kOutput, calls=%fused_computation.16 | convolution fusion | flops 805699584 | bytes 3407872 | tf_op jit(solution)/shard_map/dot_general | solution.py:215
  185.4 2.3 copy.57
  187.7 3.6 %fusion.17 = bf16[1,512,768]{1,2,0:T(8,128)(2,1)} fusion(bf16[1024,768]{1,0:T(8,128)(2,1)} %all-gather.12.cloned.1.call-done, bf16[1024,512]{1,0:T(8,128)(2,1)} %bitcast.57), kind=kOutput, calls=%fused_computation.17 | convolution fusion | flops 805699584 | bytes 3407872 | tf_op jit(solution)/shard_map/dot_general | solution.py:216
  191.3 2.3 copy.58
  193.6 51.4 %reduce-scatter.2.cloned.1.call-done = bf16[32,2048]{1,0:T(8,128)(2,1)} async-done(((bf16[256,2048]{1,0:T(8,128)(2,1)}), bf16[32,2048]{1,0:T(8,128)(2,1)}) %reduce-scatter.2.cloned.1.call-update) | async-done | bytes 131088 | tf_op jit(solution)/shard_map/reduce_scatter | solution.py:199
  (40 shorter events, 7.5 us)
Async XLA Ops:
  7.2 46.0 %copy-start = (bf16[1,2048,768]{2,1,0:T(8,128)(2,1)S(1)}, bf16[1,2048,768]{2,1,0:T(8,128)(2,1)}, u32[]{:S(2)}) copy-start(bf16[1,2048,768]{2,1,0:T(8,128)(2,1)} %param.11) | copy-start | bytes 9437188
  7.2 46.0 %all-gather.8.cloned.1.call-start = ((), (), s32[]{:S(2)}) async-start(), calls=%async_computation.6 | async-start | bytes 1179648 | tf_op jit(solution)/shard_map/all_gather | solution.py:181
  7.9 86.4 %all-gather.6.cloned.1.call-start = ((), (), s32[]{:S(2)}) async-start(), calls=%async_computation.5 | async-start | bytes 1179648 | tf_op jit(solution)/shard_map/all_gather | solution.py:182
  8.7 169.6 %all-gather.14.cloned.1.call-start = ((), (), s32[]{:S(2)}) async-start(), calls=%async_computation.10 | async-start | bytes 1966080 | tf_op jit(solution)/shard_map/all_gather | solution.py:212
  53.2 3.2 %copy-start.3 = (bf16[1,2048,768]{2,1,0:T(8,128)(2,1)S(1)}, bf16[1,2048,768]{2,1,0:T(8,128)(2,1)}, u32[]{:S(2)}) copy-start(bf16[1,2048,768]{2,1,0:T(8,128)(2,1)} %param.12) | copy-start | bytes 9437188
  53.2 3.2 %copy-start.5 = (bf16[256,2048]{1,0:T(8,128)(2,1)S(1)}, bf16[256,2048]{1,0:T(8,128)(2,1)}, u32[]{:S(2)}) copy-start(bf16[256,2048]{1,0:T(8,128)(2,1)} %all-gather.8.cloned.1.call-done) | copy-start | bytes 3145732
  58.2 44.8 %copy-start.7 = (bf16[32,8]{0,1:T(8,128)(2,1)S(1)}, bf16[32,8]{0,1:T(8,128)(2,1)}, u32[]{:S(2)}) copy-start(bf16[32,8]{0,1:T(8,128)(2,1)} %param.10) | copy-start | bytes 1540
  58.3 51.2 %copy-start.6 = (s32[32,8]{0,1:T(8,128)S(1)}, s32[32,8]{0,1:T(8,128)}, u32[]{:S(2)}) copy-start(s32[32,8]{0,1:T(8,128)} %param.9) | copy-start | bytes 3076
  99.7 9.7 %all-to-all-start.1 = ((bf16[8,1,32]{2,1,0:T(2,128)(2,1)}), bf16[8,1,32]{2,1,0:T(2,128)(2,1)S(1)}, u32[]{:S(2)}, u32[]{:S(2)}) async-start(bf16[8,1,32]{2,1,0:T(2,128)(2,1)} %convert_element_type.112), calls=%async_computation.2 | async-start | bytes 8192 | tf_op jit(solution)/shard_map/all_to_all | solution.py:202
  103.0 78.8 %all-gather.10.cloned.1.call-start = ((), (), s32[]{:S(2)}) async-start(), calls=%async_computation.8 | async-start | bytes 1966080 | tf_op jit(solution)/shard_map/all_gather | solution.py:213
  121.9 65.8 %all-gather.12.cloned.1.call-start = ((), (), s32[]{:S(2)}) async-start(), calls=%async_computation.9 | async-start | bytes 1966080 | tf_op jit(solution)/shard_map/all_gather | solution.py:214
  124.8 6.7 %copy-start.2 = (bf16[256,768]{1,0:T(8,128)(2,1)S(1)}, bf16[256,768]{1,0:T(8,128)(2,1)}, u32[]{:S(2)}) copy-start(bf16[256,768]{1,0:T(8,128)(2,1)} %get-tuple-element.40) | copy-start | bytes 1179652
  124.8 23.9 %all-to-all-start.2 = ((bf16[256,4,512]{0,2,1:T(8,128)(2,1)}), bf16[256,4,512]{0,2,1:T(8,128)(2,1)}, u32[]{:S(2)}, u32[]{:S(2)}) async-start(bf16[256,4,512]{0,2,1:T(8,128)(2,1)} %bitcast.54), calls=%async_computation.3 | async-start | bytes 2097152 | tf_op jit(solution)/shard_map/all_to_all | solution.py:210
  129.2 115.7 %reduce-scatter.2.cloned.1.call-start = ((), (), s32[]{:S(2)}) async-start(), calls=%async_computation.7 | async-start | bytes 1179648 | tf_op jit(solution)/shard_map/reduce_scatter | solution.py:199
  131.5 1.0 copy-start.1
  131.5 2.0 copy-start.4
  148.8 27.2 %all-to-all-start.3 = ((bf16[256,4,512]{0,2,1:T(8,128)(2,1)}), bf16[256,4,512]{0,2,1:T(8,128)(2,1)}, u32[]{:S(2)}, u32[]{:S(2)}) async-start(bf16[256,4,512]{0,2,1:T(8,128)(2,1)} %bitcast.55), calls=%async_computation.4 | async-start | bytes 2097152 | tf_op jit(solution)/shard_map/all_to_all | solution.py:211
Sparse Core Ops, SparseCore 0:
  10.1 42.9 all-gather.7
  55.3 38.9 all-gather.5
  99.1 18.3 all-gather.13
  122.0 21.9 all-gather.9
  145.4 31.4 all-gather.11
  180.8 64.1 reduce-scatter.1

commit v2 on v0

--- a/solution.py
+++ b/solution.py
@@ -1,6 +1,8 @@
 import jax
 import jax.numpy as jnp
 from jax import lax
+from jax.experimental import pallas as pl
+from jax.experimental.pallas import tpu as pltpu
 from jax.sharding import PartitionSpec as P
 
 block_rows = 128
@@ -63,7 +65,7 @@
     return lax.fori_loop(0, block_count, step, init)
 
 
-def body(tokens, cotangent, expert_ids, route_weights, w_gate, w_up, w_down):
+def routed_body(tokens, cotangent, expert_ids, route_weights, w_gate, w_up, w_down):
     tok_count, topk = expert_ids.shape
     model = tokens.shape[1]
     experts = lax.axis_size("ep")
@@ -150,6 +152,347 @@
         summed[1].astype(jnp.bfloat16),
         summed[2].astype(jnp.bfloat16),
     )
+
+
+def dense_weights(expert_ids, route_weights, experts):
+    named = expert_ids[:, :, None] == jnp.arange(experts, dtype=jnp.int32)[None, None, :]
+    weights = route_weights.astype(jnp.float32)[:, :, None]
+    return jnp.sum(jnp.where(named, weights, 0.0), axis=1)
+
+
+def pick_route(table, expert_ids):
+    experts = table.shape[0]
+    named = expert_ids[:, :, None] == jnp.arange(experts, dtype=jnp.int32)[None, None, :]
+    spread = table.astype(jnp.float32).T[:, None, :]
+    return jnp.sum(jnp.where(named, spread, 0.0), axis=2).astype(jnp.bfloat16)
+
+
+def fused_kernel(
+    tok_hbm, cot_hbm, wd_ref, wg_hbm, wu_hbm, wdn_hbm,
+    gt_ref, route_ref, gg_ref, gu_ref, gd_ref,
+    wg, wu, wdn, tc, wbuf, cols, colst, h_own, h_recv, part, ys, yr, zs, zr, rs, rr,
+    l_sem, w_send, w_recv, g_send, g_recv, c_send, c_recv,
+    h_send, h_recv_sem, y_send, y_recv, z_send, z_recv, r_send, r_recv,
+):
+    ep_size = lax.axis_size("ep")
+    groups = lax.axis_size("dp")
+    count = tok_hbm.shape[0]
+    col = tc.shape[3]
+    tiles, _, rows, ft = h_own.shape
+    nz = ep_size // 2
+    half = rows // 2
+    ep = lax.axis_index("ep")
+    dp = lax.axis_index("dp")
+    z, y = ep // 2, ep % 2
+    xx, core = dp // 2, dp % 2
+    mine = y * nz + z
+    ynb = z * 2 + 1 - y
+    peers_dp = (xx * 2 + 1 - core, (1 - xx) * 2 + core, (1 - xx) * 2 + 1 - core)
+    f32 = jnp.float32
+    bf16 = jnp.bfloat16
+
+    def span(index, size):
+        return pl.ds(pl.multiple_of(index * size, size), size)
+
+    def remote(src, dst, send, recv, ep_to, dp_to):
+        return pltpu.make_async_remote_copy(
+            src_ref=src, dst_ref=dst, send_sem=send, recv_sem=recv,
+            device_id=(ep_to, dp_to), device_id_type=pl.DeviceIdType.MESH,
+        )
+
+    loads = [
+        pltpu.make_async_copy(ref.at[:, pl.ds(j * col, col)], tc.at[k, j, span(mine, count)], l_sem.at[k, j])
+        for k, ref in enumerate((tok_hbm, cot_hbm))
+        for j in range(groups)
+    ]
+    for load in loads:
+        load.start()
+    own_w = pltpu.make_async_copy(wd_ref.at[ep], wbuf.at[mine], l_sem.at[2, 0])
+    own_w.start()
+    w_loads = [
+        pltpu.make_async_copy(src, dst, l_sem.at[2, 1 + k])
+        for k, (src, dst) in enumerate(((wg_hbm, wg), (wu_hbm, wu), (wdn_hbm, wdn)))
+    ]
+
+    barrier = pltpu.get_barrier_semaphore()
+    for k in range(1, ep_size):
+        pl.semaphore_signal(
+            barrier, inc=1, device_id=((ep + k) % ep_size, dp), device_id_type=pl.DeviceIdType.MESH
+        )
+    for peer in peers_dp:
+        pl.semaphore_signal(barrier, inc=1, device_id=(ep, peer), device_id_type=pl.DeviceIdType.MESH)
+    pl.semaphore_wait(barrier, ep_size - 1 + len(peers_dp))
+
+    pending = []
+
+    def go(copy):
+        copy.start()
+        pending.append(copy)
+
+    def block(which, pos):
+        return tc.at[which, :, span(pos, count)]
+
+    def send_block(which, pos, ep_to, slot):
+        go(remote(block(which, pos), block(which, pos), g_send.at[which, slot], g_recv.at[which, pos], ep_to, dp))
+
+    def wait_block(which, pos):
+        remote(block(which, pos), block(which, pos), g_send.at[which, 0], g_recv.at[which, pos], ep, dp).wait_recv()
+
+    def send_cols(which, pos):
+        for r, peer in enumerate(peers_dp):
+            remote(
+                tc.at[which, peer, span(pos, count)],
+                cols.at[which, r, span(pos, count)],
+                c_send.at[which, r], c_recv.at[which, r], ep, peer,
+            ).start()
+
+    for load in loads[:groups]:
+        load.wait()
+    for k in range(1, nz):
+        send_block(0, mine, ((z + k) % nz) * 2 + y, k - 1)
+    send_block(0, mine, ynb, nz - 1)
+    for load in loads[groups:]:
+        load.wait()
+    for k in range(1, nz):
+        send_block(1, mine, ((z + k) % nz) * 2 + y, k - 1)
+    send_block(1, mine, ynb, nz - 1)
+    for k in range(1, ep_size):
+        to = (ep + k) % ep_size
+        go(remote(wd_ref.at[to], wbuf.at[mine], w_send.at[k], w_recv.at[mine], to, dp))
+    for load in w_loads:
+        load.start()
+    send_cols(0, mine)
+    for k in range(1, nz):
+        pos = y * nz + (z + k) % nz
+        wait_block(0, pos)
+        send_block(0, pos, ynb, nz - 1 + k)
+        send_cols(0, pos)
+    for k in range(nz):
+        pos = (1 - y) * nz + (z + k) % nz
+        wait_block(0, pos)
+        send_cols(0, pos)
+    send_cols(1, mine)
+    for k in range(1, nz):
+        pos = y * nz + (z + k) % nz
+        wait_block(1, pos)
+        send_block(1, pos, ynb, nz - 1 + k)
+        send_cols(1, pos)
+    own_w.wait()
+    for k in range(1, ep_size):
+        frm = (ep + k) % ep_size
+        pos = (frm % 2) * nz + frm // 2
+        remote(wd_ref.at[frm], wbuf.at[pos], w_send.at[k], w_recv.at[pos], ep, dp).wait_recv()
+    for load in w_loads:
+        load.wait()
+    for k in range(nz):
+        pos = (1 - y) * nz + (z + k) % nz
+        wait_block(1, pos)
+        send_cols(1, pos)
+
+    weight = wbuf[...].reshape(rows, wbuf.shape[2])[:, 0:1]
+
+    def tile_step(t, route):
+        lanes = span(t, ft)
+        gate_pre = jnp.zeros((rows, ft), f32)
+        up_pre = jnp.zeros((rows, ft), f32)
+        back = jnp.zeros((rows, ft), f32)
+        for j in range(groups):
+            depth = pl.ds(j * col, col)
+            gate_pre += jnp.dot(tc[0, j], wg[depth, lanes], preferred_element_type=f32)
+            up_pre += jnp.dot(tc[0, j], wu[depth, lanes], preferred_element_type=f32)
+            back += lax.dot_general(tc[1, j], wdn[lanes, depth], contract_last, preferred_element_type=f32)
+        act, slope = silu_parts(gate_pre)
+        product = act * up_pre
+        scaled = weight * back
+        h_own[t, 0] = (scaled * up_pre * slope).astype(bf16)
+        h_own[t, 1] = (scaled * act).astype(bf16)
+        h_own[t, 2] = (weight * product).astype(bf16)
+        route = route + jnp.sum(product.astype(bf16).astype(f32) * back, axis=1, keepdims=True)
+        for r in (1, 0):
+            remote(
+                h_own.at[t], h_recv.at[r, t], h_send.at[r, t], h_recv_sem.at[r, t], ep, peers_dp[r]
+            ).start()
+        return route
+
+    route = lax.fori_loop(0, tiles, tile_step, jnp.zeros((rows, 1), f32))
+    rs[...] = jnp.broadcast_to(route, (rows, rs.shape[2])).reshape(rs.shape)
+
+    def slot_step(n, carry):
+        total = jnp.zeros((rows, col), f32)
+        for t in range(tiles):
+            lanes = pl.ds(t * ft, ft)
+            total += lax.dot_general(h_own[t, 0], wg[span(n, col), lanes], contract_last, preferred_element_type=f32)
+            total += lax.dot_general(h_own[t, 1], wu[span(n, col), lanes], contract_last, preferred_element_type=f32)
+        part[n] = total.reshape(2, half, col)
+        ys[n] = part[n, 1 - y].astype(bf16)
+        remote(ys.at[n], yr.at[n], y_send.at[n], y_recv.at[n], ynb, dp).start()
+        return carry
+
+    lax.fori_loop(0, groups, slot_step, 0)
+    for k in range(1, ep_size):
+        to = (ep + k) % ep_size
+        pos = (to % 2) * nz + to // 2
+        go(remote(rs.at[pos], rr.at[ep], r_send.at[k], r_recv.at[ep], to, dp))
+
+    colst[0] = tc[0, dp].T
+    for r in range(3):
+        remote(cols.at[0, r], cols.at[0, r], c_send.at[0, r], c_recv.at[0, r], ep, peers_dp[r]).wait_recv()
+        colst[1 + r] = cols[0, r].T
+
+    def forward(t):
+        remote(h_own.at[t], h_recv.at[1, t], h_send.at[1, t], h_recv_sem.at[1, t], ep, peers_dp[1]).wait_recv()
+        remote(
+            h_recv.at[1, t], h_recv.at[2, t], h_send.at[2, t], h_recv_sem.at[2, t], ep, peers_dp[0]
+        ).start()
+
+    def add_step(n, carry):
+        remote(ys.at[n], yr.at[n], y_send.at[n], y_recv.at[n], ynb, dp).wait()
+        total = part[n, y] + yr[n].astype(f32)
+        part[n, y] = total
+        zs[n] = total.astype(bf16)
+        for k in range(1, nz):
+            to = (z + k) % nz
+            remote(
+                zs.at[n, span(to, count)], zr.at[n, k - 1], z_send.at[n, k - 1], z_recv.at[n, k - 1], to * 2 + y, dp
+            ).start()
+        return carry
+
+    lax.fori_loop(0, groups, add_step, 0)
+    forward(0)
+    for r in range(3):
+        remote(cols.at[1, r], cols.at[1, r], c_send.at[1, r], c_recv.at[1, r], ep, peers_dp[r]).wait_recv()
+
+    def sum_step(n, carry):
+        total = part[n, y, span(z, count), :]
+        for k in range(1, nz):
+            remote(
+                zs.at[n, pl.ds(0, count)], zr.at[n, k - 1], z_send.at[n, k - 1], z_recv.at[n, k - 1], ep, dp
+            ).wait()
+            total = total + zr[n, k - 1].astype(f32)
+        gt_ref[:, span(n, col)] = total.astype(bf16)
+        return carry
+
+    def weight_step(t, carry):
+        @pl.when(t + 1 < tiles)
+        def _():
+            forward(t + 1)
+
+        @pl.when(t + 1 == tiles)
+        def _():
+            lax.fori_loop(0, groups, sum_step, 0)
+
+        for r in (0, 2):
+            remote(h_own.at[t], h_recv.at[r, t], h_send.at[r, t], h_recv_sem.at[r, t], ep, peers_dp[0]).wait_recv()
+        blocks = [h_own.at[t]] + [h_recv.at[r, t] for r in range(3)]
+        cots = [tc.at[1, dp]] + [cols.at[1, r] for r in range(3)]
+        grad_gate = jnp.zeros((col, ft), f32)
+        grad_up = jnp.zeros((col, ft), f32)
+        grad_down = jnp.zeros((ft, col), f32)
+        for g in range(4):
+            grad_gate += jnp.dot(colst[g], blocks[g][0], preferred_element_type=f32)
+            grad_up += jnp.dot(colst[g], blocks[g][1], preferred_element_type=f32)
+            grad_down += lax.dot_general(blocks[g][2], cots[g][...], contract_first, preferred_element_type=f32)
+        gg_ref[:, span(t, ft)] = grad_gate.astype(bf16)
+        gu_ref[:, span(t, ft)] = grad_up.astype(bf16)
+        gd_ref[span(t, ft), :] = grad_down.astype(bf16)
+        return carry
+
+    lax.fori_loop(0, tiles, weight_step, 0)
+
+    for k in range(1, ep_size):
+        frm = (ep + k) % ep_size
+        remote(rs.at[0], rr.at[frm], r_send.at[k], r_recv.at[frm], ep, dp).wait_recv()
+        route_ref[frm] = rr[frm]
+    route_ref[ep] = rs[mine]
+    for copy in pending:
+        copy.wait_send()
+    for which in range(2):
+        for r in range(3):
+            remote(cols.at[which, r], cols.at[which, r], c_send.at[which, r], c_recv.at[which, r], ep, peers_dp[r]).wait_send()
+    for t in range(tiles):
+        for r in range(3):
+            remote(h_own.at[t], h_recv.at[r, t], h_send.at[r, t], h_recv_sem.at[r, t], ep, peers_dp[r]).wait_send()
+
+
+def fused_body(tokens, cotangent, expert_ids, route_weights, w_gate, w_up, w_down):
+    count, topk = expert_ids.shape
+    model = tokens.shape[1]
+    experts = lax.axis_size("ep")
+    groups = lax.axis_size("dp")
+    width = w_gate.shape[2]
+    rows = experts * count
+    col = model // groups
+    ft = 256 if width % 256 == 0 else width
+    tiles = width // ft
+    lanes = 128
+    bf16 = jnp.bfloat16
+    weights = dense_weights(expert_ids, route_weights, experts)
+    spread = jnp.broadcast_to(weights.T[:, :, None], (experts, count, lanes))
+    any_spec = pl.BlockSpec(memory_space=pl.ANY)
+    vmem = pl.BlockSpec(memory_space=pltpu.VMEM)
+    dma = pltpu.SemaphoreType.DMA
+    nz = experts // 2
+    outs = pl.pallas_call(
+        fused_kernel,
+        name="fused_layer",
+        out_shape=(
+            jax.ShapeDtypeStruct((count, model), bf16),
+            jax.ShapeDtypeStruct((experts, count, lanes), jnp.float32),
+            jax.ShapeDtypeStruct((col, width), bf16),
+            jax.ShapeDtypeStruct((col, width), bf16),
+            jax.ShapeDtypeStruct((width, col), bf16),
+        ),
+        in_specs=[any_spec, any_spec, vmem, any_spec, any_spec, any_spec],
+        out_specs=(vmem,) * 5,
+        scratch_shapes=[
+            pltpu.VMEM((model, width), bf16),
+            pltpu.VMEM((model, width), bf16),
+            pltpu.VMEM((width, model), bf16),
+            pltpu.VMEM((2, groups, rows, col), bf16),
+            pltpu.VMEM((experts, count, lanes), jnp.float32),
+            pltpu.VMEM((2, 3, rows, col), bf16),
+            pltpu.VMEM((4, col, rows), bf16),
+            pltpu.VMEM((tiles, 3, rows, ft), bf16),
+            pltpu.VMEM((3, tiles, 3, rows, ft), bf16),
+            pltpu.VMEM((groups, 2, rows // 2, col), jnp.float32),
+            pltpu.VMEM((groups, rows // 2, col), bf16),
+            pltpu.VMEM((groups, rows // 2, col), bf16),
+            pltpu.VMEM((groups, rows // 2, col), bf16),
+            pltpu.VMEM((groups, nz - 1, count, col), bf16),
+            pltpu.VMEM((experts, count, lanes), jnp.float32),
+            pltpu.VMEM((experts, count, lanes), jnp.float32),
+            dma((3, max(groups, 4))),
+            dma((experts,)),
+            dma((experts,)),
+            dma((2, 2 * nz)),
+            dma((2, experts)),
+            dma((2, 3)),
+            dma((2, 3)),
+            dma((3, tiles)),
+            dma((3, tiles)),
+            dma((groups,)),
+            dma((groups,)),
+            dma((groups, nz - 1)),
+            dma((groups, nz - 1)),
+            dma((experts,)),
+            dma((experts,)),
+        ],
+        compiler_params=pltpu.CompilerParams(
+            collective_id=0, has_side_effects=True, vmem_limit_bytes=60 * 1024 * 1024
+        ),
+    )(tokens, cotangent, spread, w_gate[0], w_up[0], w_down[0])
+    grad_tokens, table, grad_gate, grad_up, grad_down = outs
+    grad_route = pick_route(table[:, :, 0], expert_ids)
+    return grad_tokens, grad_route, grad_gate[None], grad_up[None], grad_down[None]
+
+
+def body(tokens, cotangent, expert_ids, route_weights, w_gate, w_up, w_down):
+    tok_count, topk = expert_ids.shape
+    experts = lax.axis_size("ep")
+    whole = 2 * tok_count * topk // experts >= tok_count
+    paired = lax.axis_size("dp") == 4 and experts % 2 == 0 and tok_count % 16 == 0
+    chosen = fused_body if whole and paired else routed_body
+    return chosen(tokens, cotangent, expert_ids, route_weights, w_gate, w_up, w_down)
 
 
 def solution(mesh):

time: 279 us -> 90.2 us (0.32)
  the two profiles are of different devices: /device:TPU:0 before, /device:TPU:13 now
where the time goes in v2:
time: 90.2 us; the launch traced here: 89.9 us
  Pallas kernels  78.8 us (87%)
  local copies, waits for them, and re-layouts  8.42 us (9%)
  other arithmetic  1.99 us (2%)
    pallas_call x1, Pallas kernels, fused_body(): pl.pallas_call(fused_kernel, name='fused_layer', out_shape=(jax.ShapeDtyp...  78.8 us
    unnamed x8, local copies, waits for them, and re-layouts  6.58 us

profile of v2, /device:TPU:13, one launch (start us, length us, event | category | flops | bytes accessed | tf_op | source)
XLA Modules:
  0.0 89.9 jit_solution(13806430476026781658)
XLA Ops:
  0.6 0.7 convert_element_type.6
  1.3 0.7 select_reduce_fusion.1
  2.0 0.8 broadcast_in_dim.45.wd_ref
  2.8 0.0 copy-start.1
  2.8 78.8 %fused_layer.1 = (bf16[32,2048]{1,0:T(8,128)(2,1)}, f32[8,32,128]{2,1,0:T(8,128)}, bf16[512,768]{1,0:T(8,128)(2,1)}, bf16[512,768]{1,0:T(8,128)(2,1)}, bf16[768,512]{1,0:T(8,128)(2,1)}) custom-call(bf16[32,2048]{1,0:T(8,128)(2,1)} %tok_hbm.1, bf16[32,2048]{1,0:T(8,128)(2,1)} %cot_hbm.1, f32[8,32,128]{2,1,0:T(8,128)} %broadcast_in_dim.45.wd_ref, ...), custom_call_target="tpu_custom_call" | custom-call | tf_op jit(solution)/shard_map/fused_layer/pallas_call | solution.py:435
  81.6 0.0 copy-start
  81.6 1.1 %slice_reduce_fusion = f32[8,32]{1,0:T(8,128)S(1)} fusion(f32[8,32,128]{2,1,0:T(8,128)} %get-tuple-element.11), kind=kLoop, calls=%fused_computation | loop fusion | bytes 2048 | tf_op jit(solution)/shard_map/slice | solution.py:485
  82.7 0.0 copy-done.1
  82.7 0.6 select_reduce_fusion
  83.3 1.6 %copy.22 = bf16[32,2048]{1,0:T(8,128)(2,1)} copy(bf16[32,2048]{1,0:T(8,128)(2,1)} %get-tuple-element.20) | data formatting | bytes 262144
  84.9 2.1 %copy.23 = bf16[1,512,768]{2,1,0:T(8,128)(2,1)} copy(bf16[1,512,768]{2,1,0:T(8,128)(2,1)} %bitcast.13) | data formatting | bytes 1572864
  87.0 2.1 %copy.24 = bf16[1,512,768]{2,1,0:T(8,128)(2,1)} copy(bf16[1,512,768]{2,1,0:T(8,128)(2,1)} %bitcast.12) | data formatting | bytes 1572864
  89.0 0.0 copy-done
  89.0 0.9 copy.25
Async XLA Ops:
  2.8 79.9 %copy-start.1 = (s32[32,8]{0,1:T(8,128)S(1)}, s32[32,8]{0,1:T(8,128)}, u32[]{:S(2)}) copy-start(s32[32,8]{0,1:T(8,128)} %param.9) | copy-start | bytes 3076
  81.6 7.4 %copy-start = (bf16[768,512]{1,0:T(8,128)(2,1)S(1)}, bf16[768,512]{1,0:T(8,128)(2,1)}, u32[]{:S(2)}) copy-start(bf16[768,512]{1,0:T(8,128)(2,1)} %get-tuple-element.14) | copy-start | bytes 2359300

commit v3 on v2

--- a/solution.py
+++ b/solution.py
@@ -154,31 +154,19 @@
     )
 
 
-def dense_weights(expert_ids, route_weights, experts):
-    named = expert_ids[:, :, None] == jnp.arange(experts, dtype=jnp.int32)[None, None, :]
-    weights = route_weights.astype(jnp.float32)[:, :, None]
-    return jnp.sum(jnp.where(named, weights, 0.0), axis=1)
-
-
-def pick_route(table, expert_ids):
-    experts = table.shape[0]
-    named = expert_ids[:, :, None] == jnp.arange(experts, dtype=jnp.int32)[None, None, :]
-    spread = table.astype(jnp.float32).T[:, None, :]
-    return jnp.sum(jnp.where(named, spread, 0.0), axis=2).astype(jnp.bfloat16)
-
-
 def fused_kernel(
-    tok_hbm, cot_hbm, wd_ref, wg_hbm, wu_hbm, wdn_hbm,
+    tok_hbm, cot_hbm, ids_ref, rw_ref, wg_hbm, wu_hbm, wdn_hbm,
     gt_ref, route_ref, gg_ref, gu_ref, gd_ref,
-    wg, wu, wdn, tc, wbuf, cols, colst, h_own, h_recv, part, ys, yr, zs, zr, rs, rr,
+    wg, wu, wdn, tc, wd, wbuf, cols, colst, act_buf, fac_buf, hid_buf, hw_own, hw_recv, gp_own, gp_recv,
+    part, ys, yr, zs, zr, rs, rr,
     l_sem, w_send, w_recv, g_send, g_recv, c_send, c_recv,
-    h_send, h_recv_sem, y_send, y_recv, z_send, z_recv, r_send, r_recv,
+    h_send, h_done, y_send, y_recv, z_send, z_recv, r_send, r_recv,
 ):
     ep_size = lax.axis_size("ep")
     groups = lax.axis_size("dp")
     count = tok_hbm.shape[0]
     col = tc.shape[3]
-    tiles, _, rows, ft = h_own.shape
+    tiles, rows, ft = hw_own.shape
     nz = ep_size // 2
     half = rows // 2
     ep = lax.axis_index("ep")
@@ -207,8 +195,6 @@
     ]
     for load in loads:
         load.start()
-    own_w = pltpu.make_async_copy(wd_ref.at[ep], wbuf.at[mine], l_sem.at[2, 0])
-    own_w.start()
     w_loads = [
         pltpu.make_async_copy(src, dst, l_sem.at[2, 1 + k])
         for k, (src, dst) in enumerate(((wg_hbm, wg), (wu_hbm, wu), (wdn_hbm, wdn)))
@@ -221,22 +207,34 @@
         )
     for peer in peers_dp:
         pl.semaphore_signal(barrier, inc=1, device_id=(ep, peer), device_id_type=pl.DeviceIdType.MESH)
+    wd[...] = jnp.zeros(wd.shape, f32)
+    rs[...] = jnp.zeros(rs.shape, f32)
+    ids = ids_ref[...]
+    values = rw_ref[...].astype(f32)
+    for e in range(ep_size):
+        line = jnp.sum(jnp.where(ids == e, values, 0.0), axis=0, keepdims=True)
+        wd[e, :, 0:count] = jnp.broadcast_to(line, (wd.shape[1], count))
     pl.semaphore_wait(barrier, ep_size - 1 + len(peers_dp))
 
-    pending = []
-
-    def go(copy):
-        copy.start()
-        pending.append(copy)
-
-    def block(which, pos):
-        return tc.at[which, :, span(pos, count)]
-
-    def send_block(which, pos, ep_to, slot):
-        go(remote(block(which, pos), block(which, pos), g_send.at[which, slot], g_recv.at[which, pos], ep_to, dp))
-
-    def wait_block(which, pos):
-        remote(block(which, pos), block(which, pos), g_send.at[which, 0], g_recv.at[which, pos], ep, dp).wait_recv()
+    def block(which, zz, yy):
+        return tc.at[which, :, span(yy * nz + zz, count)]
+
+    def block_copy(which, way, zz, ep_to):
+        view = block(which, zz, y)
+        return remote(view, view, g_send.at[which, way, zz], g_recv.at[which, y * nz + zz], ep_to, dp)
+
+    def send_up(which, zz):
+        @pl.when(z + 1 < nz)
+        def _():
+            block_copy(which, 0, zz, ep + 2).start()
+
+    def send_down(which, zz):
+        @pl.when(z > 0)
+        def _():
+            block_copy(which, 1, zz, ep - 2).start()
+
+    def send_side(which, zz):
+        block_copy(which, 2, zz, ynb).start()
 
     def send_cols(which, pos):
         for r, peer in enumerate(peers_dp):
@@ -246,83 +244,119 @@
                 c_send.at[which, r], c_recv.at[which, r], ep, peer,
             ).start()
 
-    for load in loads[:groups]:
-        load.wait()
-    for k in range(1, nz):
-        send_block(0, mine, ((z + k) % nz) * 2 + y, k - 1)
-    send_block(0, mine, ynb, nz - 1)
-    for load in loads[groups:]:
-        load.wait()
-    for k in range(1, nz):
-        send_block(1, mine, ((z + k) % nz) * 2 + y, k - 1)
-    send_block(1, mine, ynb, nz - 1)
+    def pass_on(which, d):
+        @pl.when(z >= d)
+        def _():
+            block_copy(which, 0, z - d, ep).wait_recv()
+            send_up(which, z - d)
+            send_side(which, z - d)
+            send_cols(which, y * nz + z - d)
+
+        @pl.when(z + d < nz)
+        def _():
+            block_copy(which, 1, z + d, ep).wait_recv()
+            send_down(which, z + d)
+            send_side(which, z + d)
+            send_cols(which, y * nz + z + d)
+
+    def take_side(which):
+        def take(k, carry):
+            zz = (z + k) % nz
+            pos = (1 - y) * nz + zz
+            view = tc.at[which, :, span(pos, count)]
+            remote(view, view, g_send.at[which, 2, zz], g_recv.at[which, pos], ep, dp).wait_recv()
+            send_cols(which, pos)
+            return carry
+
+        lax.fori_loop(0, nz, take, 0)
+
+    def h_copy(kind, r, t, forwarded=False):
+        own, got = ((hw_own, hw_recv), (gp_own, gp_recv))[kind]
+        src = got.at[1, t] if forwarded else own.at[t]
+        peer = peers_dp[0] if forwarded else peers_dp[r]
+        return remote(src, got.at[r, t], h_send.at[kind, r, t], h_done.at[kind, r, t], ep, peer)
+
+    def forward(kind, t):
+        h_copy(kind, 1, t).wait_recv()
+        h_copy(kind, 2, t, True).start()
+
+    for which in range(2):
+        for load in loads[which * groups:(which + 1) * groups]:
+            load.wait()
+        send_up(which, z)
+        send_down(which, z)
+        send_side(which, z)
+        if which == 0:
+            send_cols(0, mine)
+    wbuf[mine] = wd[ep]
     for k in range(1, ep_size):
         to = (ep + k) % ep_size
-        go(remote(wd_ref.at[to], wbuf.at[mine], w_send.at[k], w_recv.at[mine], to, dp))
+        remote(wd.at[to], wbuf.at[mine], w_send.at[k], w_recv.at[mine], to, dp).start()
     for load in w_loads:
         load.start()
-    send_cols(0, mine)
-    for k in range(1, nz):
-        pos = y * nz + (z + k) % nz
-        wait_block(0, pos)
-        send_block(0, pos, ynb, nz - 1 + k)
-        send_cols(0, pos)
-    for k in range(nz):
-        pos = (1 - y) * nz + (z + k) % nz
-        wait_block(0, pos)
-        send_cols(0, pos)
-    send_cols(1, mine)
-    for k in range(1, nz):
-        pos = y * nz + (z + k) % nz
-        wait_block(1, pos)
-        send_block(1, pos, ynb, nz - 1 + k)
-        send_cols(1, pos)
-    own_w.wait()
+    for d in range(1, nz):
+        pass_on(0, d)
+    take_side(0)
     for k in range(1, ep_size):
         frm = (ep + k) % ep_size
         pos = (frm % 2) * nz + frm // 2
-        remote(wd_ref.at[frm], wbuf.at[pos], w_send.at[k], w_recv.at[pos], ep, dp).wait_recv()
+        remote(wd.at[frm], wbuf.at[pos], w_send.at[k], w_recv.at[pos], ep, dp).wait_recv()
     for load in w_loads:
         load.wait()
-    for k in range(nz):
-        pos = (1 - y) * nz + (z + k) % nz
-        wait_block(1, pos)
-        send_cols(1, pos)
-
-    weight = wbuf[...].reshape(rows, wbuf.shape[2])[:, 0:1]
-
-    def tile_step(t, route):
-        lanes = span(t, ft)
-        gate_pre = jnp.zeros((rows, ft), f32)
-        up_pre = jnp.zeros((rows, ft), f32)
+    flat = wbuf[...].reshape(ep_size * wbuf.shape[1], wbuf.shape[2])
+    turned = jnp.concatenate([flat] * (128 // flat.shape[0]), axis=0).T
+    step = wbuf.shape[1]
+    weight = jnp.concatenate([turned[0:count, p * step:p * step + 1] for p in range(ep_size)], axis=0)
+
+    for t in range(max(tiles, nz - 1)):
+        if t < nz - 1:
+            pass_on(1, t + 1)
+        if t == 0:
+            send_cols(1, mine)
+        if t < tiles:
+            lanes = pl.ds(t * ft, ft)
+            gate_pre = jnp.zeros((rows, ft), f32)
+            up_pre = jnp.zeros((rows, ft), f32)
+            for j in range(groups):
+                depth = pl.ds(j * col, col)
+                gate_pre += jnp.dot(tc[0, j], wg[depth, lanes], preferred_element_type=f32)
+                up_pre += jnp.dot(tc[0, j], wu[depth, lanes], preferred_element_type=f32)
+            act, slope = silu_parts(gate_pre)
+            product = act * up_pre
+            hw_own[t] = (weight * product).astype(bf16)
+            act_buf[t] = act
+            fac_buf[t] = up_pre * slope
+            hid_buf[t] = product.astype(bf16)
+            for r in (1, 0):
+                h_copy(0, r, t).start()
+    take_side(1)
+
+    def back_step(t, route):
         back = jnp.zeros((rows, ft), f32)
         for j in range(groups):
-            depth = pl.ds(j * col, col)
-            gate_pre += jnp.dot(tc[0, j], wg[depth, lanes], preferred_element_type=f32)
-            up_pre += jnp.dot(tc[0, j], wu[depth, lanes], preferred_element_type=f32)
-            back += lax.dot_general(tc[1, j], wdn[lanes, depth], contract_last, preferred_element_type=f32)
-        act, slope = silu_parts(gate_pre)
-        product = act * up_pre
+            back += lax.dot_general(
+                tc[1, j], wdn[span(t, ft), pl.ds(j * col, col)], contract_last, preferred_element_type=f32
+            )
         scaled = weight * back
-        h_own[t, 0] = (scaled * up_pre * slope).astype(bf16)
-        h_own[t, 1] = (scaled * act).astype(bf16)
-        h_own[t, 2] = (weight * product).astype(bf16)
-        route = route + jnp.sum(product.astype(bf16).astype(f32) * back, axis=1, keepdims=True)
+        gp_own[t, 0] = (scaled * fac_buf[t]).astype(bf16)
+        gp_own[t, 1] = (scaled * act_buf[t]).astype(bf16)
+        route = route + jnp.sum(hid_buf[t].astype(f32) * back, axis=1, keepdims=True)
         for r in (1, 0):
-            remote(
-                h_own.at[t], h_recv.at[r, t], h_send.at[r, t], h_recv_sem.at[r, t], ep, peers_dp[r]
-            ).start()
+            h_copy(1, r, t).start()
         return route
 
-    route = lax.fori_loop(0, tiles, tile_step, jnp.zeros((rows, 1), f32))
-    rs[...] = jnp.broadcast_to(route, (rows, rs.shape[2])).reshape(rs.shape)
+    route = lax.fori_loop(0, tiles, back_step, jnp.zeros((rows, 1), f32))
+    lined = jnp.broadcast_to(route, (rows, 128)).T
+    for p in range(ep_size):
+        line = lined[0:1, p * count:(p + 1) * count]
+        rs[p, :, 0:count] = jnp.broadcast_to(line, (rs.shape[1], count))
 
     def slot_step(n, carry):
         total = jnp.zeros((rows, col), f32)
         for t in range(tiles):
             lanes = pl.ds(t * ft, ft)
-            total += lax.dot_general(h_own[t, 0], wg[span(n, col), lanes], contract_last, preferred_element_type=f32)
-            total += lax.dot_general(h_own[t, 1], wu[span(n, col), lanes], contract_last, preferred_element_type=f32)
+            total += lax.dot_general(gp_own[t, 0], wg[span(n, col), lanes], contract_last, preferred_element_type=f32)
+            total += lax.dot_general(gp_own[t, 1], wu[span(n, col), lanes], contract_last, preferred_element_type=f32)
         part[n] = total.reshape(2, half, col)
         ys[n] = part[n, 1 - y].astype(bf16)
         remote(ys.at[n], yr.at[n], y_send.at[n], y_recv.at[n], ynb, dp).start()
@@ -332,18 +366,10 @@
     for k in range(1, ep_size):
         to = (ep + k) % ep_size
         pos = (to % 2) * nz + to // 2
-        go(remote(rs.at[pos], rr.at[ep], r_send.at[k], r_recv.at[ep], to, dp))
-
-    colst[0] = tc[0, dp].T
-    for r in range(3):
-        remote(cols.at[0, r], cols.at[0, r], c_send.at[0, r], c_recv.at[0, r], ep, peers_dp[r]).wait_recv()
-        colst[1 + r] = cols[0, r].T
-
-    def forward(t):
-        remote(h_own.at[t], h_recv.at[1, t], h_send.at[1, t], h_recv_sem.at[1, t], ep, peers_dp[1]).wait_recv()
-        remote(
-            h_recv.at[1, t], h_recv.at[2, t], h_send.at[2, t], h_recv_sem.at[2, t], ep, peers_dp[0]
-        ).start()
+        remote(rs.at[pos], rr.at[ep], r_send.at[k], r_recv.at[ep], to, dp).start()
+    rr[ep] = rs[mine]
+    for t in range(tiles):
+        forward(0, t)
 
     def add_step(n, carry):
         remote(ys.at[n], yr.at[n], y_send.at[n], y_recv.at[n], ynb, dp).wait()
@@ -358,9 +384,26 @@
         return carry
 
     lax.fori_loop(0, groups, add_step, 0)
-    forward(0)
+    colst[0] = tc[0, dp].T
+    for r in range(3):
+        remote(cols.at[0, r], cols.at[0, r], c_send.at[0, r], c_recv.at[0, r], ep, peers_dp[r]).wait_recv()
+        colst[1 + r] = cols[0, r].T
     for r in range(3):
         remote(cols.at[1, r], cols.at[1, r], c_send.at[1, r], c_recv.at[1, r], ep, peers_dp[r]).wait_recv()
+    forward(1, 0)
+
+    def down_step(t, carry):
+        for r in (0, 2):
+            h_copy(0, r, t).wait_recv()
+        blocks = [hw_own.at[t]] + [hw_recv.at[r, t] for r in range(3)]
+        cots = [tc.at[1, dp]] + [cols.at[1, r] for r in range(3)]
+        grad_down = jnp.zeros((ft, col), f32)
+        for g in range(4):
+            grad_down += lax.dot_general(blocks[g][...], cots[g][...], contract_first, preferred_element_type=f32)
+        gd_ref[span(t, ft), :] = grad_down.astype(bf16)
+        return carry
+
+    lax.fori_loop(0, tiles, down_step, 0)
 
     def sum_step(n, carry):
         total = part[n, y, span(z, count), :]
@@ -375,43 +418,61 @@
     def weight_step(t, carry):
         @pl.when(t + 1 < tiles)
         def _():
-            forward(t + 1)
+            forward(1, t + 1)
 
         @pl.when(t + 1 == tiles)
         def _():
             lax.fori_loop(0, groups, sum_step, 0)
 
         for r in (0, 2):
-            remote(h_own.at[t], h_recv.at[r, t], h_send.at[r, t], h_recv_sem.at[r, t], ep, peers_dp[0]).wait_recv()
-        blocks = [h_own.at[t]] + [h_recv.at[r, t] for r in range(3)]
-        cots = [tc.at[1, dp]] + [cols.at[1, r] for r in range(3)]
+            h_copy(1, r, t).wait_recv()
+        blocks = [gp_own.at[t]] + [gp_recv.at[r, t] for r in range(3)]
         grad_gate = jnp.zeros((col, ft), f32)
         grad_up = jnp.zeros((col, ft), f32)
-        grad_down = jnp.zeros((ft, col), f32)
         for g in range(4):
             grad_gate += jnp.dot(colst[g], blocks[g][0], preferred_element_type=f32)
             grad_up += jnp.dot(colst[g], blocks[g][1], preferred_element_type=f32)
-            grad_down += lax.dot_general(blocks[g][2], cots[g][...], contract_first, preferred_element_type=f32)
         gg_ref[:, span(t, ft)] = grad_gate.astype(bf16)
         gu_ref[:, span(t, ft)] = grad_up.astype(bf16)
-        gd_ref[span(t, ft), :] = grad_down.astype(bf16)
         return carry
 
     lax.fori_loop(0, tiles, weight_step, 0)
 
     for k in range(1, ep_size):
         frm = (ep + k) % ep_size
-        remote(rs.at[0], rr.at[frm], r_send.at[k], r_recv.at[frm], ep, dp).wait_recv()
-        route_ref[frm] = rr[frm]
-    route_ref[ep] = rs[mine]
-    for copy in pending:
-        copy.wait_send()
+        remote(rs.at[0], rr.at[frm], r_send.at[k], r_recv.at[frm], ep, dp).wait()
+        remote(wd.at[0], wbuf.at[mine], w_send.at[k], w_recv.at[mine], ep, dp).wait_send()
+    table = jnp.zeros(ids.shape, f32)
+    for e in range(ep_size):
+        table = table + jnp.where(ids == e, rr[e, 0:1, 0:count], 0.0)
+    route_ref[...] = table.astype(bf16)
     for which in range(2):
+        for zz in range(nz):
+            block_copy(which, 2, zz, ep).wait_send()
+
+            @pl.when(jnp.logical_and(z >= zz, z + 1 < nz))
+            def _():
+                block_copy(which, 0, zz, ep).wait_send()
+
+            @pl.when(jnp.logical_and(z <= zz, z > 0))
+            def _():
+                block_copy(which, 1, zz, ep).wait_send()
+
         for r in range(3):
             remote(cols.at[which, r], cols.at[which, r], c_send.at[which, r], c_recv.at[which, r], ep, peers_dp[r]).wait_send()
-    for t in range(tiles):
-        for r in range(3):
-            remote(h_own.at[t], h_recv.at[r, t], h_send.at[r, t], h_recv_sem.at[r, t], ep, peers_dp[r]).wait_send()
+        for t in range(tiles):
+            for r in range(3):
+                h_copy(which, r, t).wait_send()
+
+
+def store_kernel(*refs):
+    sems = refs[-1]
+    each = (len(refs) - 1) // 2
+    copies = [pltpu.make_async_copy(refs[k], refs[each + k], sems.at[k]) for k in range(each)]
+    for copy in copies:
+        copy.start()
+    for copy in copies:
+        copy.wait()
 
 
 def fused_body(tokens, cotangent, expert_ids, route_weights, w_gate, w_up, w_down):
@@ -426,50 +487,51 @@
     tiles = width // ft
     lanes = 128
     bf16 = jnp.bfloat16
-    weights = dense_weights(expert_ids, route_weights, experts)
-    spread = jnp.broadcast_to(weights.T[:, :, None], (experts, count, lanes))
+    f32 = jnp.float32
     any_spec = pl.BlockSpec(memory_space=pl.ANY)
     vmem = pl.BlockSpec(memory_space=pltpu.VMEM)
     dma = pltpu.SemaphoreType.DMA
     nz = experts // 2
+    small = (experts, 8, lanes)
+    shapes = ((count, model), (topk, count), (col, width), (col, width), (width, col))
     outs = pl.pallas_call(
         fused_kernel,
         name="fused_layer",
-        out_shape=(
-            jax.ShapeDtypeStruct((count, model), bf16),
-            jax.ShapeDtypeStruct((experts, count, lanes), jnp.float32),
-            jax.ShapeDtypeStruct((col, width), bf16),
-            jax.ShapeDtypeStruct((col, width), bf16),
-            jax.ShapeDtypeStruct((width, col), bf16),
-        ),
-        in_specs=[any_spec, any_spec, vmem, any_spec, any_spec, any_spec],
+        out_shape=tuple(pltpu.VMEM(shape, bf16) for shape in shapes),
+        in_specs=[any_spec, any_spec, vmem, vmem, any_spec, any_spec, any_spec],
         out_specs=(vmem,) * 5,
         scratch_shapes=[
             pltpu.VMEM((model, width), bf16),
             pltpu.VMEM((model, width), bf16),
             pltpu.VMEM((width, model), bf16),
             pltpu.VMEM((2, groups, rows, col), bf16),
-            pltpu.VMEM((experts, count, lanes), jnp.float32),
+            pltpu.VMEM(small, f32),
+            pltpu.VMEM(small, f32),
             pltpu.VMEM((2, 3, rows, col), bf16),
             pltpu.VMEM((4, col, rows), bf16),
-            pltpu.VMEM((tiles, 3, rows, ft), bf16),
-            pltpu.VMEM((3, tiles, 3, rows, ft), bf16),
-            pltpu.VMEM((groups, 2, rows // 2, col), jnp.float32),
+            pltpu.VMEM((tiles, rows, ft), f32),
+            pltpu.VMEM((tiles, rows, ft), f32),
+            pltpu.VMEM((tiles, rows, ft), bf16),
+            pltpu.VMEM((tiles, rows, ft), bf16),
+            pltpu.VMEM((3, tiles, rows, ft), bf16),
+            pltpu.VMEM((tiles, 2, rows, ft), bf16),
+            pltpu.VMEM((3, tiles, 2, rows, ft), bf16),
+            pltpu.VMEM((groups, 2, rows // 2, col), f32),
             pltpu.VMEM((groups, rows // 2, col), bf16),
             pltpu.VMEM((groups, rows // 2, col), bf16),
             pltpu.VMEM((groups, rows // 2, col), bf16),
             pltpu.VMEM((groups, nz - 1, count, col), bf16),
-            pltpu.VMEM((experts, count, lanes), jnp.float32),
-            pltpu.VMEM((experts, count, lanes), jnp.float32),
+            pltpu.VMEM(small, f32),
+            pltpu.VMEM(small, f32),
             dma((3, max(groups, 4))),
             dma((experts,)),
             dma((experts,)),
-            dma((2, 2 * nz)),
+            dma((2, 3, nz)),
             dma((2, experts)),
             dma((2, 3)),
             dma((2, 3)),
-            dma((3, tiles)),
-            dma((3, tiles)),
+            dma((2, 3, tiles)),
+            dma((2, 3, tiles)),
             dma((groups,)),
             dma((groups,)),
             dma((groups, nz - 1)),
@@ -478,19 +540,26 @@
             dma((experts,)),
         ],
         compiler_params=pltpu.CompilerParams(
-            collective_id=0, has_side_effects=True, vmem_limit_bytes=60 * 1024 * 1024
+            collective_id=0, has_side_effects=True, vmem_limit_bytes=48 * 1024 * 1024
         ),
-    )(tokens, cotangent, spread, w_gate[0], w_up[0], w_down[0])
-    grad_tokens, table, grad_gate, grad_up, grad_down = outs
-    grad_route = pick_route(table[:, :, 0], expert_ids)
-    return grad_tokens, grad_route, grad_gate[None], grad_up[None], grad_down[None]
+    )(tokens, cotangent, expert_ids.T, route_weights.T, w_gate[0], w_up[0], w_down[0])
+    outs = pl.pallas_call(
+        store_kernel,
+        name="store_results",
+        out_shape=tuple(jax.ShapeDtypeStruct(shape, bf16) for shape in shapes),
+        in_specs=[vmem] * 5,
+        out_specs=(any_spec,) * 5,
+        scratch_shapes=[dma((5,))],
+    )(*outs)
+    grad_tokens, grad_route, grad_gate, grad_up, grad_down = outs
+    return grad_tokens, grad_route.T, grad_gate[None], grad_up[None], grad_down[None]
 
 
 def body(tokens, cotangent, expert_ids, route_weights, w_gate, w_up, w_down):
     tok_count, topk = expert_ids.shape
     experts = lax.axis_size("ep")
     whole = 2 * tok_count * topk // experts >= tok_count
-    paired = lax.axis_size("dp") == 4 and experts % 2 == 0 and tok_count % 16 == 0
+    paired = lax.axis_size("dp") == 4 and experts in (4, 8, 16) and tok_count in (16, 32, 64, 128)
     chosen = fused_body if whole and paired else routed_body
     return chosen(tokens, cotangent, expert_ids, route_weights, w_gate, w_up, w_down)
 

time: 90.2 us -> 80.1 us (0.89)
  the two profiles are of different devices: /device:TPU:13 before, /device:TPU:0 now
where the time goes in v3:
time: 80.1 us; the launch traced here: 79.6 us
  Pallas kernels  70 us (87%)
  local copies, waits for them, and re-layouts  8.94 us (11%)
    pallas_call x1, Pallas kernels, fused_body(): pl.pallas_call(fused_kernel, name='fused_layer', out_shape=tuple((pltpu.V...  66.9 us
    unnamed x20, local copies, waits for them, and re-layouts  8.94 us
    pallas_call x1, Pallas kernels, fused_body(): pl.pallas_call(store_kernel, name='store_results', out_shape=tuple((jax.S...  3.13 us

profile of v3, /device:TPU:0, one launch (start us, length us, event | category | flops | bytes accessed | tf_op | source)
XLA Modules:
  0.0 79.6 jit_solution(175666809310867012)
XLA Ops:
  0.6 0.0 copy-start
  0.6 1.9 %copy-done = bf16[1,2048,768]{2,1,0:T(8,128)(2,1)S(1)} copy-done((bf16[1,2048,768]{2,1,0:T(8,128)(2,1)S(1)}, bf16[1,2048,768]{2,1,0:T(8,128)(2,1)}, u32[]{:S(2)}) %copy-start) | copy-done | bytes 3145752
  2.5 0.0 copy-start.4
  2.5 0.9 %copy-done.4 = bf16[32,2048]{1,0:T(8,128)(2,1)S(1)} copy-done((bf16[32,2048]{1,0:T(8,128)(2,1)S(1)}, bf16[32,2048]{1,0:T(8,128)(2,1)}, u32[]{:S(2)}) %copy-start.4) | copy-done | bytes 131096
  3.4 0.0 copy-start.5
  3.4 0.9 %copy-done.5 = bf16[32,2048]{1,0:T(8,128)(2,1)S(1)} copy-done((bf16[32,2048]{1,0:T(8,128)(2,1)S(1)}, bf16[32,2048]{1,0:T(8,128)(2,1)}, u32[]{:S(2)}) %copy-start.5) | copy-done | bytes 131096
  4.3 0.0 copy-start.7
  4.3 0.7 copy-done.7
  5.0 0.0 copy-start.8
  5.0 0.7 copy-done.8
  5.7 66.9 %fused_layer.1 = (bf16[32,2048]{1,0:T(8,128)(2,1)S(1)}, bf16[8,32]{1,0:T(8,128)(2,1)S(1)}, bf16[512,768]{1,0:T(8,128)(2,1)S(1)}, bf16[512,768]{1,0:T(8,128)(2,1)S(1)}, bf16[768,512]{1,0:T(8,128)(2,1)S(1)}) custom-call(bf16[32,2048]{1,0:T(8,128)(2,1)S(1)} %copy-done.4, bf16[32,2048]{1,0:T(8,128)(2,1)S(1)} %copy-done.5, s32[8,32]{1,0:T(8,128)S(1)} %bitcast.10, ...), custom_call_target="tpu_custom_call" | custom-call | tf_op jit(solution)/shard_map/fused_layer/pallas_call | solution.py:497
  72.6 0.0 copy-start.1
  72.6 0.9 %copy-done.1 = bf16[512,768]{1,0:T(8,128)(2,1)} copy-done((bf16[512,768]{1,0:T(8,128)(2,1)}, bf16[512,768]{1,0:T(8,128)(2,1)S(1)}, u32[]{:S(2)}) %copy-start.1) | copy-done | bytes 786456
  73.5 0.0 copy-start.2
  73.5 0.9 %copy-done.2 = bf16[512,768]{1,0:T(8,128)(2,1)} copy-done((bf16[512,768]{1,0:T(8,128)(2,1)}, bf16[512,768]{1,0:T(8,128)(2,1)S(1)}, u32[]{:S(2)}) %copy-start.2) | copy-done | bytes 786456
  74.4 0.0 copy-start.3
  74.4 0.9 %copy-done.3 = bf16[768,512]{1,0:T(8,128)(2,1)} copy-done((bf16[768,512]{1,0:T(8,128)(2,1)}, bf16[768,512]{1,0:T(8,128)(2,1)S(1)}, u32[]{:S(2)}) %copy-start.3) | copy-done | bytes 786456
  75.3 0.0 copy-start.6
  75.3 0.6 copy-done.6
  75.9 0.0 copy-start.9
  75.9 0.6 copy-done.9
  76.5 3.1 %store_results.1 = (bf16[32,2048]{1,0:T(8,128)(2,1)}, bf16[8,32]{1,0:T(8,128)(2,1)}, bf16[512,768]{1,0:T(8,128)(2,1)}, bf16[512,768]{1,0:T(8,128)(2,1)}, bf16[768,512]{1,0:T(8,128)(2,1)}) custom-call(bf16[32,2048]{1,0:T(8,128)(2,1)} %copy-done.6, bf16[8,32]{1,0:T(8,128)(2,1)} %copy-done.9, bf16[512,768]{1,0:T(8,128)(2,1)} %copy-done.1, ...), custom_call_target="tpu_custom_call" | custom-call | tf_op jit(solution)/shard_map/store_results/pallas_call | solution.py:546
Async XLA Ops:
  0.6 1.9 %copy-start = (bf16[1,2048,768]{2,1,0:T(8,128)(2,1)S(1)}, bf16[1,2048,768]{2,1,0:T(8,128)(2,1)}, u32[]{:S(2)}) copy-start(bf16[1,2048,768]{2,1,0:T(8,128)(2,1)} %param.11) | copy-start | bytes 9437188
  2.5 0.9 %copy-start.4 = (bf16[32,2048]{1,0:T(8,128)(2,1)S(1)}, bf16[32,2048]{1,0:T(8,128)(2,1)}, u32[]{:S(2)}) copy-start(bf16[32,2048]{1,0:T(8,128)(2,1)} %tok_hbm.1) | copy-start | bytes 393220
  3.4 0.9 %copy-start.5 = (bf16[32,2048]{1,0:T(8,128)(2,1)S(1)}, bf16[32,2048]{1,0:T(8,128)(2,1)}, u32[]{:S(2)}) copy-start(bf16[32,2048]{1,0:T(8,128)(2,1)} %cot_hbm.1) | copy-start | bytes 393220
  4.3 0.7 copy-start.7
  5.0 0.7 copy-start.8
  72.6 0.9 %copy-start.1 = (bf16[512,768]{1,0:T(8,128)(2,1)}, bf16[512,768]{1,0:T(8,128)(2,1)S(1)}, u32[]{:S(2)}) copy-start(bf16[512,768]{1,0:T(8,128)(2,1)S(1)} %get-tuple-element.17.refs_2_) | copy-start | bytes 2359300
  73.5 0.9 %copy-start.2 = (bf16[512,768]{1,0:T(8,128)(2,1)}, bf16[512,768]{1,0:T(8,128)(2,1)S(1)}, u32[]{:S(2)}) copy-start(bf16[512,768]{1,0:T(8,128)(2,1)S(1)} %get-tuple-element.18.refs_3_) | copy-start | bytes 2359300
  74.4 0.9 %copy-start.3 = (bf16[768,512]{1,0:T(8,128)(2,1)}, bf16[768,512]{1,0:T(8,128)(2,1)S(1)}, u32[]{:S(2)}) copy-start(bf16[768,512]{1,0:T(8,128)(2,1)S(1)} %get-tuple-element.19.refs_4_) | copy-start | bytes 2359300
  75.3 0.6 copy-start.6
  75.9 0.6 copy-start.9

commit v4 on v3

--- a/solution.py
+++ b/solution.py
@@ -155,9 +155,9 @@
 
 
 def fused_kernel(
-    tok_hbm, cot_hbm, ids_ref, rw_ref, wg_hbm, wu_hbm, wdn_hbm,
+    tok_hbm, cot_hbm, ids_hbm, rw_hbm, wg_hbm, wu_hbm, wdn_hbm,
     gt_ref, route_ref, gg_ref, gu_ref, gd_ref,
-    wg, wu, wdn, tc, wd, wbuf, cols, colst, act_buf, fac_buf, hid_buf, hw_own, hw_recv, gp_own, gp_recv,
+    ids_ref, rw_ref, wg, wu, wdn, tc, wd, wbuf, cols, colst, act_buf, fac_buf, hid_buf, hw_own, hw_recv, gp_own, gp_recv,
     part, ys, yr, zs, zr, rs, rr,
     l_sem, w_send, w_recv, g_send, g_recv, c_send, c_recv,
     h_send, h_done, y_send, y_recv, z_send, z_recv, r_send, r_recv,
@@ -195,6 +195,12 @@
     ]
     for load in loads:
         load.start()
+    lists = (
+        pltpu.make_async_copy(ids_hbm, ids_ref, l_sem.at[3, 0]),
+        pltpu.make_async_copy(rw_hbm, rw_ref, l_sem.at[3, 1]),
+    )
+    for load in lists:
+        load.start()
     w_loads = [
         pltpu.make_async_copy(src, dst, l_sem.at[2, 1 + k])
         for k, (src, dst) in enumerate(((wg_hbm, wg), (wu_hbm, wu), (wdn_hbm, wdn)))
@@ -209,6 +215,8 @@
         pl.semaphore_signal(barrier, inc=1, device_id=(ep, peer), device_id_type=pl.DeviceIdType.MESH)
     wd[...] = jnp.zeros(wd.shape, f32)
     rs[...] = jnp.zeros(rs.shape, f32)
+    for load in lists:
+        load.wait()
     ids = ids_ref[...]
     values = rw_ref[...].astype(f32)
     for e in range(ep_size):
@@ -217,6 +225,8 @@
     pl.semaphore_wait(barrier, ep_size - 1 + len(peers_dp))
 
     def block(which, zz, yy):
+        if which == 2:
+            return cols.at[1, pl.ds(1, 2), span(yy * nz + zz, count)]
         return tc.at[which, :, span(yy * nz + zz, count)]
 
     def block_copy(which, way, zz, ep_to):
@@ -236,8 +246,10 @@
     def send_side(which, zz):
         block_copy(which, 2, zz, ynb).start()
 
-    def send_cols(which, pos):
-        for r, peer in enumerate(peers_dp):
+    def send_cols(which, pos, reach=3):
+        if which == 2:
+            return
+        for r, peer in enumerate(peers_dp[:reach]):
             remote(
                 tc.at[which, peer, span(pos, count)],
                 cols.at[which, r, span(pos, count)],
@@ -250,22 +262,22 @@
             block_copy(which, 0, z - d, ep).wait_recv()
             send_up(which, z - d)
             send_side(which, z - d)
-            send_cols(which, y * nz + z - d)
+            send_cols(which, y * nz + z - d, 3 - 2 * which)
 
         @pl.when(z + d < nz)
         def _():
             block_copy(which, 1, z + d, ep).wait_recv()
             send_down(which, z + d)
             send_side(which, z + d)
-            send_cols(which, y * nz + z + d)
+            send_cols(which, y * nz + z + d, 3 - 2 * which)
 
     def take_side(which):
         def take(k, carry):
             zz = (z + k) % nz
             pos = (1 - y) * nz + zz
-            view = tc.at[which, :, span(pos, count)]
+            view = block(which, zz, 1 - y)
             remote(view, view, g_send.at[which, 2, zz], g_recv.at[which, pos], ep, dp).wait_recv()
-            send_cols(which, pos)
+            send_cols(which, pos, 3 - 2 * which)
             return carry
 
         lax.fori_loop(0, nz, take, 0)
@@ -286,8 +298,7 @@
         send_up(which, z)
         send_down(which, z)
         send_side(which, z)
-        if which == 0:
-            send_cols(0, mine)
+        send_cols(which, mine)
     wbuf[mine] = wd[ep]
     for k in range(1, ep_size):
         to = (ep + k) % ep_size
@@ -311,8 +322,6 @@
     for t in range(max(tiles, nz - 1)):
         if t < nz - 1:
             pass_on(1, t + 1)
-        if t == 0:
-            send_cols(1, mine)
         if t < tiles:
             lanes = pl.ds(t * ft, ft)
             gate_pre = jnp.zeros((rows, ft), f32)
@@ -329,7 +338,14 @@
             hid_buf[t] = product.astype(bf16)
             for r in (1, 0):
                 h_copy(0, r, t).start()
+    for r in (1, 2):
+        view = cols.at[1, r, span(mine, count)]
+        remote(view, view, c_send.at[1, r], c_recv.at[1, r], ep, peers_dp[r]).wait_recv()
+    send_up(2, z)
+    send_down(2, z)
     take_side(1)
+    send_side(2, z)
+    pass_on(2, 1)
 
     def back_step(t, route):
         back = jnp.zeros((rows, ft), f32)
@@ -346,6 +362,8 @@
         return route
 
     route = lax.fori_loop(0, tiles, back_step, jnp.zeros((rows, 1), f32))
+    for d in range(2, nz):
+        pass_on(2, d)
     lined = jnp.broadcast_to(route, (rows, 128)).T
     for p in range(ep_size):
         line = lined[0:1, p * count:(p + 1) * count]
@@ -388,8 +406,8 @@
     for r in range(3):
         remote(cols.at[0, r], cols.at[0, r], c_send.at[0, r], c_recv.at[0, r], ep, peers_dp[r]).wait_recv()
         colst[1 + r] = cols[0, r].T
-    for r in range(3):
-        remote(cols.at[1, r], cols.at[1, r], c_send.at[1, r], c_recv.at[1, r], ep, peers_dp[r]).wait_recv()
+    remote(cols.at[1, 0], cols.at[1, 0], c_send.at[1, 0], c_recv.at[1, 0], ep, peers_dp[0]).wait_recv()
+    take_side(2)
     forward(1, 0)
 
     def down_step(t, carry):
@@ -446,7 +464,7 @@
     for e in range(ep_size):
         table = table + jnp.where(ids == e, rr[e, 0:1, 0:count], 0.0)
     route_ref[...] = table.astype(bf16)
-    for which in range(2):
+    for which in range(3):
         for zz in range(nz):
             block_copy(which, 2, zz, ep).wait_send()
 
@@ -458,8 +476,10 @@
             def _():
                 block_copy(which, 1, zz, ep).wait_send()
 
+    for which in range(2):
         for r in range(3):
-            remote(cols.at[which, r], cols.at[which, r], c_send.at[which, r], c_recv.at[which, r], ep, peers_dp[r]).wait_send()
+            view = cols.at[1, r, span(mine, count)] if which == 1 and r > 0 else cols.at[which, r]
+            remote(view, view, c_send.at[which, r], c_recv.at[which, r], ep, peers_dp[r]).wait_send()
         for t in range(tiles):
             for r in range(3):
                 h_copy(which, r, t).wait_send()
@@ -489,6 +509,7 @@
     bf16 = jnp.bfloat16
     f32 = jnp.float32
     any_spec = pl.BlockSpec(memory_space=pl.ANY)
+    hbm = pl.BlockSpec(memory_space=pltpu.HBM)
     vmem = pl.BlockSpec(memory_space=pltpu.VMEM)
     dma = pltpu.SemaphoreType.DMA
     nz = experts // 2
@@ -498,9 +519,11 @@
         fused_kernel,
         name="fused_layer",
         out_shape=tuple(pltpu.VMEM(shape, bf16) for shape in shapes),
-        in_specs=[any_spec, any_spec, vmem, vmem, any_spec, any_spec, any_spec],
+        in_specs=[hbm] * 7,
         out_specs=(vmem,) * 5,
         scratch_shapes=[
+            pltpu.VMEM((topk, count), jnp.int32),
+            pltpu.VMEM((topk, count), bf16),
             pltpu.VMEM((model, width), bf16),
             pltpu.VMEM((model, width), bf16),
             pltpu.VMEM((width, model), bf16),
@@ -523,11 +546,11 @@
             pltpu.VMEM((groups, nz - 1, count, col), bf16),
             pltpu.VMEM(small, f32),
             pltpu.VMEM(small, f32),
-            dma((3, max(groups, 4))),
+            dma((4, max(groups, 4))),
             dma((experts,)),
             dma((experts,)),
-            dma((2, 3, nz)),
-            dma((2, experts)),
+            dma((3, 3, nz)),
+            dma((3, experts)),
             dma((2, 3)),
             dma((2, 3)),
             dma((2, 3, tiles)),
@@ -540,16 +563,17 @@
             dma((experts,)),
         ],
         compiler_params=pltpu.CompilerParams(
-            collective_id=0, has_side_effects=True, vmem_limit_bytes=48 * 1024 * 1024
+            collective_id=0, has_side_effects=True, vmem_limit_bytes=64200000
         ),
     )(tokens, cotangent, expert_ids.T, route_weights.T, w_gate[0], w_up[0], w_down[0])
     outs = pl.pallas_call(
         store_kernel,
         name="store_results",
         out_shape=tuple(jax.ShapeDtypeStruct(shape, bf16) for shape in shapes),
-        in_specs=[vmem] * 5,
+        in_specs=[any_spec] * 5,
         out_specs=(any_spec,) * 5,
         scratch_shapes=[dma((5,))],
+        compiler_params=pltpu.CompilerParams(vmem_limit_bytes=4 * 1024 * 1024),
     )(*outs)
     grad_tokens, grad_route, grad_gate, grad_up, grad_down = outs
     return grad_tokens, grad_route.T, grad_gate[None], grad_up[None], grad_down[None]

time: 80.1 us -> 60.8 us (0.76)
  Pallas kernels: 70 us -> 59.9 us
  local copies, waits for them, and re-layouts: 8.94 us -> 0 us
    unnamed x20 -> x0, local copies, waits for them, and re-layouts: 8.94 us -> none
    pallas_call x1, Pallas kernels: 66.9 us -> 58.5 us  [fused_body(): pl.pallas_call(fused_kernel, name='fused_layer', out_shape=tuple((pltpu.V...]
    pallas_call x1, Pallas kernels: 3.13 us -> 1.49 us  [fused_body(): pl.pallas_call(store_kernel, name='store_results', out_shape=tuple((jax.S...]
where the time goes in v4:
time: 60.8 us; the launch traced here: 60.6 us
  Pallas kernels  59.9 us (99%)
  between operations  0.64 us (1%)
    pallas_call x1, Pallas kernels, fused_body(): pl.pallas_call(fused_kernel, name='fused_layer', out_shape=tuple((pltpu.V...  58.5 us
    pallas_call x1, Pallas kernels, fused_body(): pl.pallas_call(store_kernel, name='store_results', out_shape=tuple((jax.S...  1.49 us

profile of v4, /device:TPU:0, one launch (start us, length us, event | category | flops | bytes accessed | tf_op | source)
XLA Modules:
  0.0 60.6 jit_solution(14149647554084327244)
XLA Ops:
  0.6 58.5 %fused_layer.1 = (bf16[32,2048]{1,0:T(8,128)(2,1)S(1)}, bf16[8,32]{1,0:T(8,128)(2,1)S(1)}, bf16[512,768]{1,0:T(8,128)(2,1)S(1)}, bf16[512,768]{1,0:T(8,128)(2,1)S(1)}, bf16[768,512]{1,0:T(8,128)(2,1)S(1)}) custom-call(bf16[32,2048]{1,0:T(8,128)(2,1)} %tok_hbm.1, bf16[32,2048]{1,0:T(8,128)(2,1)} %cot_hbm.1, s32[8,32]{1,0:T(8,128)} %bitcast.12, ...), custom_call_target="tpu_custom_call" | custom-call | tf_op jit(solution)/shard_map/fused_layer/pallas_call | solution.py:518
  59.1 1.5 %store_results.1 = (bf16[32,2048]{1,0:T(8,128)(2,1)}, bf16[8,32]{1,0:T(8,128)(2,1)}, bf16[512,768]{1,0:T(8,128)(2,1)}, bf16[512,768]{1,0:T(8,128)(2,1)}, bf16[768,512]{1,0:T(8,128)(2,1)}) custom-call(bf16[32,2048]{1,0:T(8,128)(2,1)S(1)} %get-tuple-element.15.refs_0_, bf16[8,32]{1,0:T(8,128)(2,1)S(1)} %get-tuple-element.16.refs_1_, ...), custom_call_target="tpu_custom_call" | custom-call | tf_op jit(solution)/shard_map/store_results/pallas_call | solution.py:569

commit v5 on v4

--- a/solution.py
+++ b/solution.py
@@ -158,7 +158,7 @@
     tok_hbm, cot_hbm, ids_hbm, rw_hbm, wg_hbm, wu_hbm, wdn_hbm,
     gt_ref, route_ref, gg_ref, gu_ref, gd_ref,
     ids_ref, rw_ref, wg, wu, wdn, tc, wd, wbuf, cols, colst, act_buf, fac_buf, hid_buf, hw_own, hw_recv, gp_own, gp_recv,
-    part, ys, yr, zs, zr, rs, rr,
+    part, ys, yr, zs, zr, rs, rr, weight_buf, route_buf,
     l_sem, w_send, w_recv, g_send, g_recv, c_send, c_recv,
     h_send, h_done, y_send, y_recv, z_send, z_recv, r_send, r_recv,
 ):
@@ -283,10 +283,15 @@
         lax.fori_loop(0, nz, take, 0)
 
     def h_copy(kind, r, t, forwarded=False):
-        own, got = ((hw_own, hw_recv), (gp_own, gp_recv))[kind]
-        src = got.at[1, t] if forwarded else own.at[t]
+        if kind == 0:
+            src = hw_recv.at[1, t] if forwarded else hw_own.at[t]
+            dst = hw_recv.at[r, t]
+        else:
+            sub = span(y if kind == 1 else 1 - y, half)
+            src = gp_recv.at[1, t, :, sub] if forwarded else gp_own.at[t, :, sub]
+            dst = gp_recv.at[r, t, :, sub]
         peer = peers_dp[0] if forwarded else peers_dp[r]
-        return remote(src, got.at[r, t], h_send.at[kind, r, t], h_done.at[kind, r, t], ep, peer)
+        return remote(src, dst, h_send.at[kind, r, t], h_done.at[kind, r, t], ep, peer)
 
     def forward(kind, t):
         h_copy(kind, 1, t).wait_recv()
@@ -318,6 +323,7 @@
     turned = jnp.concatenate([flat] * (128 // flat.shape[0]), axis=0).T
     step = wbuf.shape[1]
     weight = jnp.concatenate([turned[0:count, p * step:p * step + 1] for p in range(ep_size)], axis=0)
+    weight_buf[...] = jnp.broadcast_to(weight, weight_buf.shape)
 
     for t in range(max(tiles, nz - 1)):
         if t < nz - 1:
@@ -338,6 +344,28 @@
             hid_buf[t] = product.astype(bf16)
             for r in (1, 0):
                 h_copy(0, r, t).start()
+    def back_rows(kind):
+        sub = span(y if kind == 1 else 1 - y, half)
+        factor = weight_buf[sub, 0:1]
+
+        def back_step(t, route):
+            back = jnp.zeros((half, ft), f32)
+            for j in range(groups):
+                back += lax.dot_general(
+                    tc[1, j, sub, :], wdn[span(t, ft), pl.ds(j * col, col)], contract_last, preferred_element_type=f32
+                )
+            scaled = factor * back
+            gp_own[t, 0, sub, :] = (scaled * fac_buf[t, sub, :]).astype(bf16)
+            gp_own[t, 1, sub, :] = (scaled * act_buf[t, sub, :]).astype(bf16)
+            route = route + jnp.sum(hid_buf[t, sub, :].astype(f32) * back, axis=1, keepdims=True)
+            for r in (1, 0):
+                h_copy(kind, r, t).start()
+            return route
+
+        route = lax.fori_loop(0, tiles, back_step, jnp.zeros((half, 1), f32))
+        route_buf[sub, :] = jnp.broadcast_to(route, (half, route_buf.shape[1]))
+
+    back_rows(1)
     for r in (1, 2):
         view = cols.at[1, r, span(mine, count)]
         remote(view, view, c_send.at[1, r], c_recv.at[1, r], ep, peers_dp[r]).wait_recv()
@@ -347,24 +375,10 @@
     send_side(2, z)
     pass_on(2, 1)
 
-    def back_step(t, route):
-        back = jnp.zeros((rows, ft), f32)
-        for j in range(groups):
-            back += lax.dot_general(
-                tc[1, j], wdn[span(t, ft), pl.ds(j * col, col)], contract_last, preferred_element_type=f32
-            )
-        scaled = weight * back
-        gp_own[t, 0] = (scaled * fac_buf[t]).astype(bf16)
-        gp_own[t, 1] = (scaled * act_buf[t]).astype(bf16)
-        route = route + jnp.sum(hid_buf[t].astype(f32) * back, axis=1, keepdims=True)
-        for r in (1, 0):
-            h_copy(1, r, t).start()
-        return route
-
-    route = lax.fori_loop(0, tiles, back_step, jnp.zeros((rows, 1), f32))
+    back_rows(2)
     for d in range(2, nz):
         pass_on(2, d)
-    lined = jnp.broadcast_to(route, (rows, 128)).T
+    lined = route_buf[...].T
     for p in range(ep_size):
         line = lined[0:1, p * count:(p + 1) * count]
         rs[p, :, 0:count] = jnp.broadcast_to(line, (rs.shape[1], count))
@@ -408,7 +422,9 @@
         colst[1 + r] = cols[0, r].T
     remote(cols.at[1, 0], cols.at[1, 0], c_send.at[1, 0], c_recv.at[1, 0], ep, peers_dp[0]).wait_recv()
     take_side(2)
-    forward(1, 0)
+    for t in range(tiles):
+        forward(1, t)
+    forward(2, 0)
 
     def down_step(t, carry):
         for r in (0, 2):
@@ -436,14 +452,15 @@
     def weight_step(t, carry):
         @pl.when(t + 1 < tiles)
         def _():
-            forward(1, t + 1)
+            forward(2, t + 1)
 
         @pl.when(t + 1 == tiles)
         def _():
             lax.fori_loop(0, groups, sum_step, 0)
 
-        for r in (0, 2):
-            h_copy(1, r, t).wait_recv()
+        for kind in (1, 2):
+            for r in (0, 2):
+                h_copy(kind, r, t).wait_recv()
         blocks = [gp_own.at[t]] + [gp_recv.at[r, t] for r in range(3)]
         grad_gate = jnp.zeros((col, ft), f32)
         grad_up = jnp.zeros((col, ft), f32)
@@ -480,9 +497,10 @@
         for r in range(3):
             view = cols.at[1, r, span(mine, count)] if which == 1 and r > 0 else cols.at[which, r]
             remote(view, view, c_send.at[which, r], c_recv.at[which, r], ep, peers_dp[r]).wait_send()
+    for kind in range(3):
         for t in range(tiles):
             for r in range(3):
-                h_copy(which, r, t).wait_send()
+                h_copy(kind, r, t).wait_send()
 
 
 def store_kernel(*refs):
@@ -546,6 +564,8 @@
             pltpu.VMEM((groups, nz - 1, count, col), bf16),
             pltpu.VMEM(small, f32),
             pltpu.VMEM(small, f32),
+            pltpu.VMEM((rows, lanes), f32),
+            pltpu.VMEM((rows, lanes), f32),
             dma((4, max(groups, 4))),
             dma((experts,)),
             dma((experts,)),
@@ -553,8 +573,8 @@
             dma((3, experts)),
             dma((2, 3)),
             dma((2, 3)),
-            dma((2, 3, tiles)),
-            dma((2, 3, tiles)),
+            dma((3, 3, tiles)),
+            dma((3, 3, tiles)),
             dma((groups,)),
             dma((groups,)),
             dma((groups, nz - 1)),

time: 60.8 us -> 62.5 us (1.028)
  Pallas kernels: 59.9 us -> 61.7 us
    pallas_call x1, Pallas kernels: 58.5 us -> 60.2 us  [fused_body(): pl.pallas_call(fused_kernel, name='fused_layer', out_shape=tuple((pltpu.V...]
where the time goes in v5:
time: 62.5 us; the launch traced here: 62.3 us
  Pallas kernels  61.7 us (99%)
  between operations  0.64 us (1%)
    pallas_call x1, Pallas kernels, fused_body(): pl.pallas_call(fused_kernel, name='fused_layer', out_shape=tuple((pltpu.V...  60.2 us
    pallas_call x1, Pallas kernels, fused_body(): pl.pallas_call(store_kernel, name='store_results', out_shape=tuple((jax.S...  1.49 us

profile of v5, /device:TPU:0, one launch (start us, length us, event | category | flops | bytes accessed | tf_op | source)
XLA Modules:
  0.0 62.3 jit_solution(14190925335028106017)
XLA Ops:
  0.6 60.2 %fused_layer.1 = (bf16[32,2048]{1,0:T(8,128)(2,1)S(1)}, bf16[8,32]{1,0:T(8,128)(2,1)S(1)}, bf16[512,768]{1,0:T(8,128)(2,1)S(1)}, bf16[512,768]{1,0:T(8,128)(2,1)S(1)}, bf16[768,512]{1,0:T(8,128)(2,1)S(1)}) custom-call(bf16[32,2048]{1,0:T(8,128)(2,1)} %tok_hbm.1, bf16[32,2048]{1,0:T(8,128)(2,1)} %cot_hbm.1, s32[8,32]{1,0:T(8,128)} %bitcast.12, ...), custom_call_target="tpu_custom_call" | custom-call | tf_op jit(solution)/shard_map/fused_layer/pallas_call | solution.py:536
  60.8 1.5 %store_results.1 = (bf16[32,2048]{1,0:T(8,128)(2,1)}, bf16[8,32]{1,0:T(8,128)(2,1)}, bf16[512,768]{1,0:T(8,128)(2,1)}, bf16[512,768]{1,0:T(8,128)(2,1)}, bf16[768,512]{1,0:T(8,128)(2,1)}) custom-call(bf16[32,2048]{1,0:T(8,128)(2,1)S(1)} %get-tuple-element.15.refs_0_, bf16[8,32]{1,0:T(8,128)(2,1)S(1)} %get-tuple-element.16.refs_1_, ...), custom_call_target="tpu_custom_call" | custom-call | tf_op jit(solution)/shard_map/store_results/pallas_call | solution.py:589

commit v6 on v5

--- a/solution.py
+++ b/solution.py
@@ -246,14 +246,14 @@
     def send_side(which, zz):
         block_copy(which, 2, zz, ynb).start()
 
-    def send_cols(which, pos, reach=3):
+    def send_cols(which, pos, reach=3, side=False):
         if which == 2:
             return
         for r, peer in enumerate(peers_dp[:reach]):
             remote(
                 tc.at[which, peer, span(pos, count)],
                 cols.at[which, r, span(pos, count)],
-                c_send.at[which, r], c_recv.at[which, r], ep, peer,
+                c_send.at[2 if side and r > 0 else which, r], c_recv.at[2 if side and r > 0 else which, r], ep, peer,
             ).start()
 
     def pass_on(which, d):
@@ -261,14 +261,16 @@
         def _():
             block_copy(which, 0, z - d, ep).wait_recv()
             send_up(which, z - d)
-            send_side(which, z - d)
+            if which < 2:
+                send_side(which, z - d)
             send_cols(which, y * nz + z - d, 3 - 2 * which)
 
         @pl.when(z + d < nz)
         def _():
             block_copy(which, 1, z + d, ep).wait_recv()
             send_down(which, z + d)
-            send_side(which, z + d)
+            if which < 2:
+                send_side(which, z + d)
             send_cols(which, y * nz + z + d, 3 - 2 * which)
 
     def take_side(which):
@@ -277,7 +279,7 @@
             pos = (1 - y) * nz + zz
             view = block(which, zz, 1 - y)
             remote(view, view, g_send.at[which, 2, zz], g_recv.at[which, pos], ep, dp).wait_recv()
-            send_cols(which, pos, 3 - 2 * which)
+            send_cols(which, pos, 3, which == 1)
             return carry
 
         lax.fori_loop(0, nz, take, 0)
@@ -372,7 +374,6 @@
     send_up(2, z)
     send_down(2, z)
     take_side(1)
-    send_side(2, z)
     pass_on(2, 1)
 
     back_rows(2)
@@ -421,7 +422,9 @@
         remote(cols.at[0, r], cols.at[0, r], c_send.at[0, r], c_recv.at[0, r], ep, peers_dp[r]).wait_recv()
         colst[1 + r] = cols[0, r].T
     remote(cols.at[1, 0], cols.at[1, 0], c_send.at[1, 0], c_recv.at[1, 0], ep, peers_dp[0]).wait_recv()
-    take_side(2)
+    for r in (1, 2):
+        view = cols.at[1, r, span(1 - y, half)]
+        remote(view, view, c_send.at[2, r], c_recv.at[2, r], ep, peers_dp[r]).wait_recv()
     for t in range(tiles):
         forward(1, t)
     forward(2, 0)
@@ -483,7 +486,8 @@
     route_ref[...] = table.astype(bf16)
     for which in range(3):
         for zz in range(nz):
-            block_copy(which, 2, zz, ep).wait_send()
+            if which < 2:
+                block_copy(which, 2, zz, ep).wait_send()
 
             @pl.when(jnp.logical_and(z >= zz, z + 1 < nz))
             def _():
@@ -497,6 +501,9 @@
         for r in range(3):
             view = cols.at[1, r, span(mine, count)] if which == 1 and r > 0 else cols.at[which, r]
             remote(view, view, c_send.at[which, r], c_recv.at[which, r], ep, peers_dp[r]).wait_send()
+    for r in (1, 2):
+        view = cols.at[1, r, span(1 - y, half)]
+        remote(view, view, c_send.at[2, r], c_recv.at[2, r], ep, peers_dp[r]).wait_send()
     for kind in range(3):
         for t in range(tiles):
             for r in range(3):
@@ -571,8 +578,8 @@
             dma((experts,)),
             dma((3, 3, nz)),
             dma((3, experts)),
-            dma((2, 3)),
-            dma((2, 3)),
+            dma((3, 3)),
+            dma((3, 3)),
             dma((3, 3, tiles)),
             dma((3, 3, tiles)),
             dma((groups,)),

time: 62.5 us -> 64 us (1.024)
  Pallas kernels: 61.7 us -> 63.2 us
    pallas_call x1, Pallas kernels: 60.2 us -> 61.7 us  [fused_body(): pl.pallas_call(fused_kernel, name='fused_layer', out_shape=tuple((pltpu.V...]
where the time goes in v6:
time: 64 us; the launch traced here: 63.8 us
  Pallas kernels  63.2 us (99%)
  between operations  0.64 us (1%)
    pallas_call x1, Pallas kernels, fused_body(): pl.pallas_call(fused_kernel, name='fused_layer', out_shape=tuple((pltpu.V...  61.7 us
    pallas_call x1, Pallas kernels, fused_body(): pl.pallas_call(store_kernel, name='store_results', out_shape=tuple((jax.S...  1.49 us

profile of v6, /device:TPU:0, one launch (start us, length us, event | category | flops | bytes accessed | tf_op | source)
XLA Modules:
  0.0 63.8 jit_solution(9984490704680843856)
XLA Ops:
  0.6 61.7 %fused_layer.1 = (bf16[32,2048]{1,0:T(8,128)(2,1)S(1)}, bf16[8,32]{1,0:T(8,128)(2,1)S(1)}, bf16[512,768]{1,0:T(8,128)(2,1)S(1)}, bf16[512,768]{1,0:T(8,128)(2,1)S(1)}, bf16[768,512]{1,0:T(8,128)(2,1)S(1)}) custom-call(bf16[32,2048]{1,0:T(8,128)(2,1)} %tok_hbm.1, bf16[32,2048]{1,0:T(8,128)(2,1)} %cot_hbm.1, s32[8,32]{1,0:T(8,128)} %bitcast.12, ...), custom_call_target="tpu_custom_call" | custom-call | tf_op jit(solution)/shard_map/fused_layer/pallas_call | solution.py:543
  62.4 1.5 %store_results.1 = (bf16[32,2048]{1,0:T(8,128)(2,1)}, bf16[8,32]{1,0:T(8,128)(2,1)}, bf16[512,768]{1,0:T(8,128)(2,1)}, bf16[512,768]{1,0:T(8,128)(2,1)}, bf16[768,512]{1,0:T(8,128)(2,1)}) custom-call(bf16[32,2048]{1,0:T(8,128)(2,1)S(1)} %get-tuple-element.15.refs_0_, bf16[8,32]{1,0:T(8,128)(2,1)S(1)} %get-tuple-element.16.refs_1_, ...), custom_call_target="tpu_custom_call" | custom-call | tf_op jit(solution)/shard_map/store_results/pallas_call | solution.py:596
